TPU v7x, 128 devices: a whole 4x4x4 slice. The times are simulated.
128 devices in a mesh: row: 8 (over x, core), col: 16 (over z, y).
Axes of the slice: x: 4, y: 4, z: 4, core: 2. Of those that a mesh axis runs over, the one named last changes fastest.
Arguments:
- trailing: float32 [24576, 24576], P('row', 'col'), may hold values from -6 to 6
- panel_first: float32 [24576, 256], P(('row', 'col')), may hold values from -0.0390625 to 0.0390625
- panel_second: float32 [24576, 256], P(('row', 'col')), may hold values from -0.0390625 to 0.0390625
- link_block: float32 [256, 256], replicated, may hold values from -0.375 to 0.375
- inverse_first: float32 [256, 256], replicated, may hold values from -6 to 6
- inverse_second: float32 [256, 256], replicated, may hold values from -6 to 6
- tile_struct: int32 [2, 192], replicated, may hold values 0 or 1
Outputs:
- panel_out_first: float32 [24576, 256], P(('row', 'col'))
- diag_out_first: float32 [256, 256], replicated
- panel_out_second: float32 [24576, 256], P(('row', 'col'))
- cross_out_second: float32 [256, 256], replicated
- diag_out_second: float32 [256, 256], replicated
All inputs are finite; a program needn't handle non-finite values.
Results may differ from a plain program's by a relative error of at most 0.000071.
Values sent between devices are 32-bit elements; how exact they have to be, the bound alone decides.
A program may use at most 128 MiB of HBM per device.

v0:
```python
import jax
import jax.numpy as jnp
from jax import lax
from jax.sharding import Mesh
from jax.sharding import PartitionSpec as P

TILE = 128
COL = ("col_0", "col_1")
ROW = ("row_0", "row_1")
ROW_COL = ("row_0", "row_1", "col_0", "col_1")


def filled_up(lines, size):
    spare = -lines.shape[0] % size
    if not spare:
        return lines
    return jnp.concatenate([lines, jnp.zeros((spare, *lines.shape[1:]), lines.dtype)])


def broadcast_by_parts(x, axis, root):
    lines = jnp.where(lax.axis_index(axis) == root, x, jnp.zeros_like(x)).reshape(
        -1, *x.shape[1:][-1:]
    )
    padded = filled_up(lines, lax.axis_size(axis))
    own = lax.psum_scatter(padded, axis, scatter_dimension=0, tiled=True)
    return lax.all_gather(own, axis, axis=0, tiled=True)[: len(lines)].reshape(x.shape)


def summed_rows(total, axes):
    for axis in axes:
        total = lax.psum_scatter(total, axis, scatter_dimension=0, tiled=True)
    return total


def in_blocks(x, dim, size):
    before, after = (x.shape[:dim], x.shape[dim + 1 :])
    return jnp.moveaxis(x.reshape(*before, size, -1, *after), dim, 0)


def sent_and_summed(x, axis, dim):
    blocks = in_blocks(x, dim, lax.axis_size(axis))
    arrived = lax.all_to_all(blocks, axis, split_axis=0, concat_axis=0, tiled=True)
    return arrived.sum(axis=0)


def sum_in_two_steps(x, axes, dim):
    far, near = axes
    own = sent_and_summed(in_blocks(x, dim, lax.axis_size(far)), near, dim + 1)
    return jnp.sum(lax.all_to_all(own, far, 0, 0, tiled=True), axis=0)


def sent_to_all(x, axis):
    size = lax.axis_size(axis)
    return lax.all_to_all(jnp.broadcast_to(x[None], (size, *x.shape)), axis, 0, 0, tiled=True)


def in_order(blocks, dim):
    blocks = jnp.moveaxis(blocks, 0, dim)
    shape = blocks.shape
    return blocks.reshape(*shape[:dim], shape[dim] * shape[dim + 1], *shape[dim + 2 :])


def gather_axes(x, axes, dim):
    far, near = axes
    leading = sent_to_all(x, far)
    blocks = jnp.swapaxes(sent_to_all(leading, near), 0, 1)
    return in_order(blocks.reshape(-1, *x.shape), dim)


def nested_sum(x, axes):
    own = sum_in_two_steps(filled_up(x, lax.axis_size(axes[0]) * lax.axis_size(axes[1])), axes, 0)
    whole = gather_axes(own, axes, 0)
    return whole[: len(x)].reshape(x.shape)


def together(arrays, axis):
    ends = [0]
    for a in arrays:
        ends.append(ends[-1] + a.size)
    total = nested_sum(jnp.concatenate([a.ravel() for a in arrays]), axis)
    return tuple((total[b:e].reshape(a.shape) for a, b, e in zip(arrays, ends, ends[1:])))


def matmul(left, right):
    return jnp.dot(left, right, precision=lax.Precision.HIGHEST, preferred_element_type=jnp.float32)


def inner(left, right):
    return lax.dot_general(
        left,
        right,
        (((0,), (0,)), ((), ())),
        precision=lax.Precision.HIGHEST,
        preferred_element_type=jnp.float32,
    )


def column_rows(block, col_index):
    half = block.shape[0] // 2
    return lax.dynamic_slice_in_dim(block, col_index % 2 * half, half, 0)


def on_device(
    trailing, panel_first, panel_second, link_block, inverse_first, inverse_second, tile_struct
):
    n_col = lax.axis_size(COL)
    row_index = lax.axis_index(ROW)
    col_index = lax.axis_index(COL)
    count = panel_first.shape[0]
    offset = (row_index * n_col + col_index) * count
    row_mask = jnp.repeat(tile_struct, TILE, axis=1)
    local_mask = lax.dynamic_slice_in_dim(row_mask, offset, count, 1).astype(jnp.float32)
    lead_first = panel_first * local_mask[0][:, None]
    lead_second = panel_second * local_mask[1][:, None]
    width = lead_first.shape[1]
    joined = jnp.concatenate([lead_first, lead_second], axis=1)
    block = lax.all_gather(joined, COL, axis=0, tiled=True)
    mine = column_rows(block, col_index)
    columns = broadcast_by_parts(mine, ROW, col_index // 2)
    products = summed_rows(matmul(trailing, columns), COL)
    first_prod = products[:, :width]
    reach = products[:, width:]
    panel_out_first = -first_prod
    panel_out_second = -(matmul(panel_out_first, link_block) + reach)
    diag_sum, cross_sum, reach_sum = together(
        (
            inner(lead_first, panel_out_first),
            inner(panel_out_first, lead_second),
            inner(lead_second, reach),
        ),
        (("row_0", "row_1", "col_0"), "col_1"),
    )
    diag_out_first = inverse_first - diag_sum
    cross_out_second = -(matmul(diag_out_first, link_block) + cross_sum)
    diag_out_second = (
        inverse_second
        - inner(link_block, cross_out_second)
        + matmul(cross_sum.T, link_block)
        + reach_sum
    )
    return (panel_out_first, diag_out_first, panel_out_second, cross_out_second, diag_out_second)


def solution(mesh):
    finer = Mesh(mesh.devices.reshape(4, 2, 4, 4), ("row_0", "row_1", "col_0", "col_1"))
    in_specs = (P(ROW, COL), P(ROW_COL, None), P(ROW_COL, None), P(), P(), P(), P())
    out_specs = (P(ROW_COL, None), P(), P(ROW_COL, None), P(), P())
    return jax.shard_map(
        on_device, mesh=finer, in_specs=in_specs, out_specs=out_specs, check_vma=False
    )
```

profile of v0, /device:TPU:1, one launch (start us, length us, event | category | flops | bytes accessed | tf_op | source)
XLA Modules:
  0.0 372.8 jit_solution(13370178319316764590)
XLA Ops:
  7.2 0.8 broadcast_bitcast_fusion
  8.3 1.1 broadcast_multiply_fusion
  9.5 0.8 pad_maximum_fusion.1
  10.4 64.5 %all-gather.3.cloned.1.call-done = f32[3072,512]{1,0:T(8,128)} async-done(((f32[192,512]{1,0:T(8,128)}), f32[3072,512]{1,0:T(8,128)}) %all-gather.3.cloned.1.call-update) | async-done | bytes 6291472 | tf_op jit(solution)/shard_map/all_gather | solution.py:117
  74.9 4.0 %dynamic-slice_select_fusion = f32[1536,512]{1,0:T(8,128)} fusion(f32[3072,512]{1,0:T(8,128)} %all-gather.3.cloned.1.call-done, s32[]{:T(128)S(6)} %select_n.29, pred[]{:T(512)S(6)} %eq.5), kind=kLoop, calls=%fused_computation.1 | loop fusion | flops 786432 | bytes 6291461 | tf_op jit(solution)/shard_map/jit(_where)/select_n | solution.py:21
  78.9 32.8 %reduce-scatter.6.cloned.1.call-done = f32[192,512]{1,0:T(8,128)} async-done(((f32[1536,512]{1,0:T(8,128)}), f32[192,512]{1,0:T(8,128)}) %reduce-scatter.6.cloned.1.call-update) | async-done | bytes 393232 | tf_op jit(solution)/shard_map/reduce_scatter | solution.py:25
  111.8 31.5 %all-gather.5.cloned.1.call-done = f32[1536,512]{1,0:T(8,128)} async-done(((f32[192,512]{1,0:T(8,128)}), f32[1536,512]{1,0:T(8,128)}) %all-gather.5.cloned.1.call-update) | async-done | bytes 3145744 | tf_op jit(solution)/shard_map/all_gather | solution.py:26
  143.3 63.6 %convolution_bitcast_fusion = f32[3072,512]{0,1:T(8,128)} fusion(f32[1536,512]{1,0:T(8,128)} %all-gather.5.cloned.1.call-done, f32[3072,1536]{1,0:T(8,128)} %param.7), kind=kOutput, calls=%fused_computation | convolution fusion | flops 28991029248 | bytes 28311552 | tf_op jit(solution)/shard_map/dot_general | solution.py:85
  206.9 63.8 %reduce-scatter.8.cloned.1.call-done = f32[768,512]{0,1:T(8,128)} async-done(((f32[3072,512]{0,1:T(8,128)}), f32[768,512]{0,1:T(8,128)}) %reduce-scatter.8.cloned.1.call-update) | async-done | bytes 1572880 | tf_op jit(solution)/shard_map/reduce_scatter | solution.py:31
  270.7 3.0 copy.26
  273.8 24.7 %reduce-scatter.10.cloned.1.call-done = f32[192,512]{1,0:T(8,128)} async-done(((f32[768,512]{1,0:T(8,128)}), f32[192,512]{1,0:T(8,128)}) %reduce-scatter.10.cloned.1.call-update) | async-done | bytes 393232 | tf_op jit(solution)/shard_map/reduce_scatter | solution.py:31
  298.4 0.9 slice.36
  299.5 0.7 convolution_bitcast_fusion.4
  300.7 1.6 convolution_bitcast_fusion.2
  303.2 13.4 %all_to_all.25 = f32[4,32,1536]{2,1,0:T(8,128)S(1)} all-to-all(f32[4,32,1536]{2,1,0:T(8,128)S(1)} %copy.21), channel_id=1, replica_groups=mesh['row_0'=4,'row_1'=2,'col_0'=4,'col_1'=4] {'col_1'}, dimensions={0} | all-to-all | bytes 1572864 | tf_op jit(solution)/shard_map/all_to_all | solution.py:42
  316.8 17.5 %all_to_all.26 = f32[32,1,1536]{2,1,0:T(1,128)S(1)} all-to-all(f32[32,1,1536]{2,1,0:T(1,128)S(1)} %all_to_all.17), channel_id=1, replica_groups=mesh['row_0'=4,'row_1'=2,'col_0'=4,'col_1'=4] {'row_0','row_1','col_0'}, dimensions={0} | all-to-all | bytes 393216 | tf_op jit(solution)/shard_map/all_to_all | solution.py:49
  334.5 12.1 %all_to_all.27 = f32[32,1,1536]{2,1,0:T(1,128)S(1)} all-to-all(f32[32,1,1536]{2,1,0:T(1,128)S(1)} %broadcast_in_dim.22), channel_id=1, replica_groups=mesh['row_0'=4,'row_1'=2,'col_0'=4,'col_1'=4] {'row_0','row_1','col_0'}, dimensions={0} | all-to-all | bytes 393216 | tf_op jit(solution)/shard_map/all_to_all | solution.py:54
  346.6 1.0 broadcast_in_dim.24
  347.5 3.6 all-to-all-start.3
  351.2 0.8 copy.24
  352.0 1.3 fusion.3
  353.3 9.7 %all-to-all-done.3 = f32[4,32,1536]{2,1,0:T(8,128)S(1)} async-done(((f32[4,32,1536]{2,1,0:T(8,128)}), f32[4,32,1536]{2,1,0:T(8,128)S(1)}, u32[]{:S(2)}, u32[]{:S(2)}) %all-to-all-start.3) | async-done | bytes 786464 | tf_op jit(solution)/shard_map/all_to_all | solution.py:54
  364.4 0.6 fusion.1
  365.0 1.3 fusion
  (43 shorter events, 3.8 us)
Async XLA Ops:
  7.2 344.8 %copy-start = (f32[256,256]{1,0:T(8,128)S(1)}, f32[256,256]{1,0:T(8,128)}, u32[]{:S(2)}) copy-start(f32[256,256]{1,0:T(8,128)} %param.10) | copy-start | bytes 786436
  7.2 67.7 %all-gather.3.cloned.1.call-start = ((), (), s32[]{:S(2)}) async-start(), calls=%async_computation.7 | async-start | bytes 6684672 | tf_op jit(solution)/shard_map/all_gather | solution.py:117
  10.3 101.4 %reduce-scatter.6.cloned.1.call-start = ((), (), s32[]{:S(2)}) async-start(), calls=%async_computation.8 | async-start | bytes 3538944 | tf_op jit(solution)/shard_map/reduce_scatter | solution.py:25
  78.9 64.4 %all-gather.5.cloned.1.call-start = ((), (), s32[]{:S(2)}) async-start(), calls=%async_computation.9 | async-start | bytes 3538944 | tf_op jit(solution)/shard_map/all_gather | solution.py:26
  111.7 159.0 %reduce-scatter.8.cloned.1.call-start = ((), (), s32[]{:S(2)}) async-start(), calls=%async_computation.10 | async-start | bytes 7864320 | tf_op jit(solution)/shard_map/reduce_scatter | solution.py:31
  206.9 91.6 %reduce-scatter.10.cloned.1.call-start = ((), (), s32[]{:S(2)}) async-start(), calls=%async_computation.11 | async-start | bytes 1966080 | tf_op jit(solution)/shard_map/reduce_scatter | solution.py:31
  316.6 35.4 %copy-start.3 = (f32[192,512]{1,0:T(8,128)S(1)}, f32[192,512]{1,0:T(8,128)}, u32[]{:S(2)}) copy-start(f32[192,512]{1,0:T(8,128)} %reduce-scatter.10.cloned.1.call-done) | copy-start | bytes 1179652
  347.5 16.4 %copy-start.4 = (f32[256,256]{1,0:T(8,128)S(1)}, f32[256,256]{1,0:T(8,128)}, u32[]{:S(2)}) copy-start(f32[256,256]{1,0:T(8,128)} %param.11) | copy-start | bytes 786436
  347.5 15.4 %all-to-all-start.3 = ((f32[4,32,1536]{2,1,0:T(8,128)}), f32[4,32,1536]{2,1,0:T(8,128)S(1)}, u32[]{:S(2)}, u32[]{:S(2)}) async-start(f32[4,32,1536]{2,1,0:T(8,128)} %broadcast_in_dim.24), calls=%async_computation.5 | async-start | bytes 1572864 | tf_op jit(solution)/shard_map/all_to_all | solution.py:54
  351.2 13.2 %copy-start.5 = (f32[256,256]{1,0:T(8,128)S(1)}, f32[256,256]{1,0:T(8,128)}, u32[]{:S(2)}) copy-start(f32[256,256]{1,0:T(8,128)} %param.12) | copy-start | bytes 786436
  363.9 2.3 copy-start.1
  364.4 1.9 copy-start.2
Sparse Core Ops, SparseCore 0:
  10.4 64.4 all-gather.2
  79.0 32.6 reduce-scatter.5
  113.4 29.8 all-gather.4
  207.0 63.6 reduce-scatter.7
  273.9 24.5 reduce-scatter.9
where the time goes:
time: 373 us
  waiting for transfers between devices  227 us (61%)
  matrix products  69.7 us (19%)
  blocking collectives  42.9 us (12%)
  between operations  14 us (4%)
  local copies, waits for them, and re-layouts  8.96 us (2%)
  other arithmetic  6.27 us (2%)
  starting transfers between devices  3.83 us (1%)
    reduce_scatter x2, waiting for transfers between devices, summed_rows(): total = lax.psum_scatter(total, axis, scatter_dimension=0, tiled=True)  88.5 us
    dot_general x4, matrix products, matmul(): jnp.dot(left, right, precision=lax.Precision.HIGHEST, preferred_element_t...  66.5 us
    all_gather x1, waiting for transfers between devices, on_device(): block = lax.all_gather(joined, COL, axis=0, tiled=True)  64.5 us
    reduce_scatter x1, waiting for transfers between devices, broadcast_by_parts(): own = lax.psum_scatter(padded, axis, scatter_dimension=0, tiled=True)  32.8 us
    all_gather x1, waiting for transfers between devices, broadcast_by_parts(): lax.all_gather(own, axis, axis=0, tiled=True)[:len(lines)].reshape(x.shape)  31.5 us
    all_to_all x1, blocking collectives, sum_in_two_steps(): return jnp.sum(lax.all_to_all(own, far, 0, 0, tiled=True), axis=0)  17.5 us
    all_to_all x1, blocking collectives, sent_and_summed(): lax.all_to_all(blocks, axis, split_axis=0, concat_axis=0, tiled=True)  13.4 us
    all_to_all x1, blocking collectives, sent_to_all(): lax.all_to_all(jnp.broadcast_to(x[None], (size, *x.shape)), axis, 0, 0, t...  12.1 us
  transfers between devices with their start and end apart: 6, of which 6 were waited for; matrix products, arithmetic and copies ran while one was open for 1% of the time, Pallas kernels for 0%

commit v1 on v0

v1 whole, which is shorter than its diff:
```python
import functools

import jax
import jax.numpy as jnp
from jax import lax
from jax.experimental import pallas as pl
from jax.experimental.pallas import tpu as pltpu
from jax.sharding import Mesh
from jax.sharding import PartitionSpec as P

AXES = ("x", "core", "z", "y")
MESH = pl.DeviceIdType.MESH
ROWS = 192
W = 256
HALF = 128
DEPTH = 1536
SUMS = 3 * W
PART = SUMS // 32

UNITS = (
    [(2, 2), (2, 3), (2, 0), (2, 1)]
    + [(3, 2), (0, 2), (1, 2)]
    + [(1, 1), (1, 3), (3, 1), (3, 3)]
    + [(1, 0), (3, 0), (0, 1), (0, 3), (0, 0)]
)
PLACE = {unit: i for i, unit in enumerate(UNITS)}


def route(near, far):
    if near == 0:
        return "keep", 0
    if near == 2:
        return "relay", 1 if far % 2 == 0 else -1
    if near == 1:
        return ("joined" if far % 2 == 0 else "own"), 1
    return ("joined" if far % 2 == 1 else "own"), -1


def split(value):
    high = value.astype(jnp.bfloat16)
    return high, (value - high.astype(jnp.float32)).astype(jnp.bfloat16)


def dot(left, right):
    return jnp.dot(left, right, preferred_element_type=jnp.float32)


def exact(left, right, contract=(1, 0)):
    return lax.dot_general(
        left,
        right,
        (((contract[0],), (contract[1],)), ((), ())),
        precision=lax.Precision.HIGHEST,
        preferred_element_type=jnp.float32,
    )


def kernel(
    struct, trailing, first, second, link_in, inv1_in, inv2_in,
    out1, diag1, out2, cross2, diag2,
    t_buf, raw, lead_h, lead_l, prod_a, prod_b, got_a, got_b, far_a, far_b,
    lead, link, inv1, inv2, y_buf,
    sums, sum_p, sum_q, sum_x, total,
    t_sem, in_sem, g1_send, g1_recv, g2_send, g2_recv, g3_send, g3_recv,
    r_send, r_recv, f_send, f_recv, s_send, s_recv,
):
    x, k, z, y = (lax.axis_index(name) for name in AXES)
    c = z * 4 + y
    flat = (x * 2 + k) * 16 + c
    panels = (first, second)

    def at(dx=0, dk=0, dz=0, dy=0):
        return (
            lax.rem(x + dx + 4, 4) if dx else x,
            1 - k if dk else k,
            lax.rem(z + dz + 4, 4) if dz else z,
            lax.rem(y + dy + 4, 4) if dy else y,
        )

    def remote(src, dst, send, recv, where):
        return pltpu.make_async_remote_copy(
            src_ref=src, dst_ref=dst, send_sem=send, recv_sem=recv, device_id=where, device_id_type=MESH
        )

    def t_copy(u, start=None):
        dy, dz = UNITS[u]
        block = lax.rem(z + dz, 4) * 4 + lax.rem(y + dy, 4)
        return pltpu.make_async_copy(
            trailing.at[pl.ds(pl.multiple_of(block * ROWS, ROWS), ROWS)], t_buf.at[u], t_sem.at[u]
        )

    own_copies = [
        pltpu.make_async_copy(first, lead.at[0], in_sem.at[0]),
        pltpu.make_async_copy(second, lead.at[1], in_sem.at[1]),
        pltpu.make_async_copy(link_in, link, in_sem.at[2]),
        pltpu.make_async_copy(inv1_in, inv1, in_sem.at[3]),
        pltpu.make_async_copy(inv2_in, inv2, in_sem.at[4]),
    ]
    for copy in own_copies:
        copy.start()
    for u in range(16):
        t_copy(u).start()

    target = [(q, lax.rem(z, 2), x, 2 * k + lax.div(z, 2)) for q in range(4)]
    source = [(z, lax.div(y, 2), 2 * lax.rem(y, 2) + k, i) for i in range(4)]
    at_home = (z == x) & (k == lax.rem(z, 2)) & (y == 2 * k + lax.div(z, 2))
    plane = [(o // 4, o % 4) for o in range(1, 16)]
    barrier = pltpu.get_barrier_semaphore()

    def greet(where):
        pl.semaphore_signal(barrier, inc=1, device_id=where, device_id_type=MESH)

    mate = at(dk=1)
    for i in range(4):
        for where, same in ((target[i], at_home & (x == i)), (source[i], at_home & (y == i))):
            greet(tuple(jnp.where(same, there, here) for there, here in zip(mate, where)))
    for dx in (1, 2, 3):
        greet(at(dx=dx))
    greet(at(dk=1))
    for dz, dy in plane:
        greet(at(dz=dz, dy=dy))
    mate_home = (z == x) & (1 - k == lax.rem(z, 2)) & (y == 2 * (1 - k) + lax.div(z, 2))
    pl.semaphore_wait(barrier, 27 + 2 * mate_home.astype(jnp.int32) - 2 * at_home.astype(jnp.int32))

    def quarter(p, q):
        slot = raw.at[p, lax.rem(z, 2) * 4 + y, pl.ds(q * 48, 48)]
        return remote(panels[p].at[pl.ds(q * 48, 48)], slot, g1_send.at[p, q], g1_recv.at[p, y], target[q])

    def quarter_home(p, q):
        slot = raw.at[p, lax.rem(z, 2) * 4 + y, pl.ds(q * 48, 48)]
        return pltpu.make_async_copy(panels[p].at[pl.ds(q * 48, 48)], slot, g1_recv.at[p, y])

    for p in range(2):
        for q in range(4):
            same = at_home & (x == q)

            @pl.when(same)
            def _(p=p, q=q):
                quarter_home(p, q).start()

            @pl.when(jnp.logical_not(same))
            def _(p=p, q=q):
                quarter(p, q).start()

    for copy in own_copies:
        copy.wait()
    for p in range(2):
        for s in range(3):
            rows = pl.ds(64 * s, 64)
            mask = struct[p, lax.div(flat * 3 + s, 2)].astype(jnp.float32)
            lead[p, rows] = lead[p, rows] * mask

    def pieces(p, lo, n, dx):
        q = lax.rem(x + dx + 4, 4)
        return raw.at[p, pl.ds(4 * k + lo, n), pl.ds(pl.multiple_of(q * 48, 48), 48)]

    def ring(p, way, m):
        step = 1 if way == 0 else -1
        lo = (0, 2, 0)[m] if way == 0 else (2, 0, 2)[m]
        ref = pieces(p, lo, 2, -step if m == 2 else 0)
        return remote(ref, ref, g2_send.at[p, way, m], g2_recv.at[p, way, m], at(dx=step))

    def ring_wait(p, way, m):
        step = 1 if way == 0 else -1
        lo = (0, 2, 0)[m] if way == 0 else (2, 0, 2)[m]
        ref = pieces(p, lo, 2, -2 * step if m == 2 else -step)
        remote(ref, ref, g2_send.at[p, way, m], g2_recv.at[p, way, m], at(dx=step)).wait_recv()

    def across(p, m):
        ref = pieces(p, 0, 4, (0, -1, 1, 2)[m])
        return remote(ref, ref, g3_send.at[p, m], g3_recv.at[p, m], at(dk=1))

    def across_wait(p, m):
        q = lax.rem(x + (0, -1, 1, 2)[m] + 4, 4)
        ref = raw.at[p, pl.ds(4 * (1 - k), 4), pl.ds(pl.multiple_of(q * 48, 48), 48)]
        remote(ref, ref, g3_send.at[p, m], g3_recv.at[p, m], at(dk=1)).wait_recv()

    def gather_1(p):
        for i in range(4):
            ref = raw.at[p, 4 * k + i, pl.ds(pl.multiple_of(x * 48, 48), 48)]
            pltpu.make_async_copy(ref, ref, g1_recv.at[p, i]).wait()
        for m in range(2):
            for way in range(2):
                ring(p, way, m).start()
        across(p, 0).start()

    def gather_2(p):
        for way in range(2):
            ring_wait(p, way, 0)
            ring(p, way, 2).start()

    def gather_3(p):
        for way in range(2):
            ring_wait(p, way, 1)
            across(p, 1 + way).start()

    def gather_4(p):
        for way in range(2):
            ring_wait(p, way, 2)
        across(p, 3).start()

    def gather_5(p):
        for m in range(4):
            across_wait(p, m)

        @pl.loop(0, 8)
        def _(j):
            for s in range(3):
                mask = struct[p, lax.div((c * 8 + j) * 3 + s, 2)].astype(jnp.float32)
                high, low = split(raw[p, j, pl.ds(64 * s, 64)] * mask)
                rows = pl.ds(pl.multiple_of(j * ROWS + 64 * s, 64), 64)
                lead_h[p, rows] = high
                lead_l[p, rows] = low

    def pick(h):
        return (prod_a, got_a, far_a) if h == 0 else (prod_b, got_b, far_b)

    def roles(h, unit):
        dy, dz = unit
        near, far = (dy, dz) if h == 0 else (dz, dy)
        return near, far, *route(near, far)

    def next_to(h, way, phase=1):
        along_y = (h == 0) == (phase == 1)
        return at(dy=way) if along_y else at(dz=way)

    def hop(p, h, unit):
        near, far, kind, way = roles(h, unit)
        prod, got, _ = pick(h)
        slot = 0 if kind == "relay" else (1 if way == 1 else 2)
        return remote(
            prod.at[p, PLACE[unit]], got.at[p, slot, far], r_send.at[p, h, slot, far], r_recv.at[p, h, slot, far],
            next_to(h, way),
        )

    def hop_wait(p, h, slot, far):
        _, got, _ = pick(h)
        ref = got.at[p, slot, far]
        remote(ref, ref, r_send.at[p, h, slot, far], r_recv.at[p, h, slot, far], next_to(h, 1)).wait_recv()

    def unit_of(h, near, far):
        return (near, far) if h == 0 else (far, near)

    def compute(p, lo, hi):
        @pl.loop(lo, hi)
        def _(u):
            if p == 0:
                for v in range(lo, hi):

                    @pl.when(u == v)
                    def _(v=v):
                        t_copy(v).wait()

            high, low = split(t_buf[u])
            wide = (dot(high, lead_h[p]) + dot(low, lead_h[p])) + dot(high, lead_l[p])
            prod_a[p, u] = wide[:, :HALF]
            prod_b[p, u] = wide[:, HALF:]
            for v in range(lo, hi):
                sends = [h for h in range(2) if roles(h, UNITS[v])[2] in ("relay", "own")]
                if sends:

                    @pl.when(u == v)
                    def _(v=v, sends=sends):
                        for h in sends:
                            hop(p, h, UNITS[v]).start()

    def joined(p, h):
        prod, got, _ = pick(h)
        for near, far in ((1, 0), (1, 2), (3, 1), (3, 3)):
            unit = unit_of(h, near, far)
            hop_wait(p, h, 0, far)
            prod[p, PLACE[unit]] = prod[p, PLACE[unit]] + got[p, 0, far]
            hop(p, h, unit).start()

    def second_send(p, h, far):
        prod, _, got = pick(h)
        return remote(
            prod.at[p, PLACE[unit_of(h, 0, far)]], got.at[p, far - 1], f_send.at[p, h, far - 1],
            f_recv.at[p, h, far - 1], next_to(h, far, phase=2),
        )

    def second_phase(p, h):
        prod, got, _ = pick(h)
        for far in (2, 1, 3, 0):
            u = PLACE[unit_of(h, 0, far)]
            hop_wait(p, h, 1, far)
            hop_wait(p, h, 2, far)
            prod[p, u] = prod[p, u] + (got[p, 1, far] + got[p, 2, far])
            if far:
                second_send(p, h, far).start()

    def finish(p, h):
        prod, _, got = pick(h)
        for far in (1, 2, 3):
            ref = got.at[p, far - 1]
            remote(ref, ref, f_send.at[p, h, far - 1], f_recv.at[p, h, far - 1], next_to(h, far, 2)).wait_recv()
        value = (prod[p, PLACE[(0, 0)]] + got[p, 0]) + (got[p, 1] + got[p, 2])
        y_buf[p, :, pl.ds(h * HALF, HALF)] = value

    def rows_of(core, place):
        return pl.ds(pl.multiple_of(core * (SUMS // 2) + place * PART, 8), PART)

    def half_of(core):
        return pl.ds(pl.multiple_of(core * (SUMS // 2), 8), SUMS // 2)

    def reduce_all():
        swap = remote(sums.at[half_of(1 - k)], sum_p, s_send.at[0], s_recv.at[0], at(dk=1))
        swap.start()
        swap.wait_recv()
        sums[half_of(k)] = sums[half_of(k)] + sum_p[...]
        for o, (dz, dy) in enumerate(plane):
            where = at(dz=dz, dy=dy)
            remote(
                sums.at[rows_of(k, where[2] * 4 + where[3])], sum_q.at[o], s_send.at[1], s_recv.at[1], where
            ).start()
        remote(sum_q, sum_q, s_send.at[1], s_recv.at[1], at(dk=1)).wait_recv()
        value = sums[rows_of(k, c)]
        for o in range(15):
            value = value + sum_q[o]
        sum_x[x] = value
        cross = [
            remote(sum_x.at[x], sum_x.at[x], s_send.at[1 + dx], s_recv.at[1 + dx], at(dx=dx)) for dx in (1, 2, 3)
        ]
        for copy in cross:
            copy.start()
        for dx in (1, 2, 3):
            ref = sum_x.at[lax.rem(x - dx + 4, 4)]
            remote(ref, ref, s_send.at[1 + dx], s_recv.at[1 + dx], at(dx=dx)).wait_recv()
        mine = rows_of(k, c)
        total[mine] = (sum_x[0] + sum_x[1]) + (sum_x[2] + sum_x[3])
        for dz, dy in plane:
            remote(total.at[mine], total.at[mine], s_send.at[5], s_recv.at[5], at(dz=dz, dy=dy)).start()
        remote(sum_q, sum_q, s_send.at[5], s_recv.at[5], at(dk=1)).wait_recv()
        back = remote(total.at[half_of(k)], total.at[half_of(k)], s_send.at[6], s_recv.at[6], at(dk=1))
        back.start()
        ref = total.at[half_of(1 - k)]
        remote(ref, ref, s_send.at[6], s_recv.at[6], at(dk=1)).wait_recv()
        swap.wait_send()
        remote(sum_q, sum_q, s_send.at[1], s_recv.at[1], at(dk=1)).wait_send()
        for copy in cross:
            copy.wait_send()
        remote(sum_q, sum_q, s_send.at[5], s_recv.at[5], at(dk=1)).wait_send()
        back.wait_send()

    gather_1(0)
    gather_2(0)
    gather_3(0)
    gather_4(0)
    gather_5(0)
    compute(0, 0, 4)
    gather_1(1)
    compute(0, 4, 7)
    gather_2(1)
    compute(0, 7, 11)
    gather_3(1)
    gather_4(1)
    compute(0, 11, 16)
    joined(0, 0)
    joined(0, 1)
    gather_5(1)
    compute(1, 0, 4)
    compute(1, 4, 7)
    second_phase(0, 0)
    compute(1, 7, 11)
    second_phase(0, 1)
    compute(1, 11, 16)
    joined(1, 0)
    joined(1, 1)
    finish(0, 0)
    finish(0, 1)
    out1[...] = -y_buf[0]
    out2[...] = exact(y_buf[0], link[...])
    for p in range(2):
        sums[pl.ds(p * W, W)] = exact(lead[p], y_buf[0], (0, 0))
    second_phase(1, 0)
    second_phase(1, 1)
    finish(1, 0)
    finish(1, 1)
    out2[...] = out2[...] - y_buf[1]
    sums[pl.ds(2 * W, W)] = exact(lead[1], y_buf[1], (0, 0))
    reduce_all()
    diag1[...] = inv1[...] + total[pl.ds(0, W)]
    cross2[...] = jnp.transpose(total[pl.ds(W, W)]) - exact(diag1[...], link[...])
    diag2[...] = (
        (inv2[...] - exact(link[...], cross2[...], (0, 0))) - exact(total[pl.ds(W, W)], link[...])
    ) + total[pl.ds(2 * W, W)]

    for p in range(2):
        for q in range(4):

            @pl.when(jnp.logical_not(at_home & (x == q)))
            def _(p=p, q=q):
                quarter(p, q).wait_send()

        for way in range(2):
            for m in range(3):
                ring(p, way, m).wait_send()
        for m in range(4):
            across(p, m).wait_send()
        for h in range(2):
            for unit in UNITS:
                if roles(h, unit)[2] != "keep":
                    hop(p, h, unit).wait_send()
            for far in (1, 2, 3):
                second_send(p, h, far).wait_send()


def on_device(trailing, first, second, link, inv1, inv2, struct):
    f32, bf16 = jnp.float32, jnp.bfloat16
    square = jax.ShapeDtypeStruct((W, W), f32)
    tall = jax.ShapeDtypeStruct((ROWS, W), f32)
    vmem, anywhere = pl.BlockSpec(memory_space=pltpu.VMEM), pl.BlockSpec(memory_space=pl.ANY)
    dma = pltpu.SemaphoreType.DMA
    block = (ROWS, HALF)
    return pl.pallas_call(
        kernel,
        out_shape=(tall, square, tall, square, square),
        in_specs=[pl.BlockSpec(memory_space=pltpu.SMEM)] + [anywhere] * 6,
        out_specs=(vmem,) * 5,
        scratch_shapes=[
            pltpu.VMEM((16, ROWS, DEPTH), f32),
            pltpu.VMEM((2, 8, ROWS, W), f32),
            pltpu.VMEM((2, DEPTH, W), bf16),
            pltpu.VMEM((2, DEPTH, W), bf16),
            pltpu.VMEM((2, 16, *block), f32),
            pltpu.VMEM((2, 16, *block), f32),
            pltpu.VMEM((2, 3, 4, *block), f32),
            pltpu.VMEM((2, 3, 4, *block), f32),
            pltpu.VMEM((2, 3, *block), f32),
            pltpu.VMEM((2, 3, *block), f32),
            pltpu.VMEM((2, ROWS, W), f32),
            pltpu.VMEM((W, W), f32),
            pltpu.VMEM((W, W), f32),
            pltpu.VMEM((W, W), f32),
            pltpu.VMEM((2, ROWS, W), f32),
            pltpu.VMEM((SUMS, W), f32),
            pltpu.VMEM((SUMS // 2, W), f32),
            pltpu.VMEM((15, PART, W), f32),
            pltpu.VMEM((4, PART, W), f32),
            pltpu.VMEM((SUMS, W), f32),
            dma((16,)), dma((5,)), dma((2, 4)), dma((2, 4)), dma((2, 2, 3)), dma((2, 2, 3)), dma((2, 4)), dma((2, 4)),
            dma((2, 2, 3, 4)), dma((2, 2, 3, 4)), dma((2, 2, 3)), dma((2, 2, 3)), dma((7,)), dma((7,)),
        ],
        compiler_params=pltpu.CompilerParams(
            collective_id=0, has_side_effects=True, vmem_limit_bytes=60 * 1024 * 1024
        ),
        name="selected_inversion",
    )(struct, trailing, first, second, link, inv1, inv2)


def solution(mesh):
    finer = Mesh(mesh.devices.reshape(4, 2, 4, 4), AXES)
    row, col = ("x", "core"), ("z", "y")
    both = (*row, *col)
    in_specs = (P(row, col), P(both, None), P(both, None), P(), P(), P(), P())
    out_specs = (P(both, None), P(), P(both, None), P(), P())
    return jax.shard_map(on_device, mesh=finer, in_specs=in_specs, out_specs=out_specs, check_vma=False)
```

time: 373 us -> 113 us (0.30)
  waiting for transfers between devices: 227 us -> 0 us
  Pallas kernels: 0 us -> 104 us
  matrix products: 69.7 us -> 0 us
  blocking collectives: 42.9 us -> 0 us
  between operations: 14 us -> 0.64 us
  other arithmetic: 6.27 us -> 0 us
  starting transfers between devices: 3.83 us -> 0 us
    reduce_scatter x3 -> x0, waiting for transfers between devices: 121 us -> none  [the longest x2 88.5 us: summed_rows(): total = lax.psum_scatter(total, axis, scatter_dimension=0, tiled=True)]
    pallas_call x0 -> x1, Pallas kernels: none -> 104 us  [on_device(): pl.pallas_call(kernel, out_shape=(tall, square, tall, square, square), in...]
    all_gather x2 -> x0, waiting for transfers between devices: 96 us -> none  [the longest x1 64.5 us: on_device(): block = lax.all_gather(joined, COL, axis=0, tiled=True)]
    dot_general x8 -> x0, matrix products: 69.7 us -> none  [the longest x4 66.5 us: matmul(): jnp.dot(left, right, precision=lax.Precision.HIGHEST, preferred_element_t...]
    all_to_all x3 -> x0, blocking collectives: 42.9 us -> none  [the longest x1 17.5 us: sum_in_two_steps(): return jnp.sum(lax.all_to_all(own, far, 0, 0, tiled=True), axis=0)]
    all_to_all x1 -> x0, waiting for transfers between devices: 9.71 us -> none  [sent_to_all(): lax.all_to_all(jnp.broadcast_to(x[None], (size, *x.shape)), axis, 0, 0, t...]
    select_n x1 -> x0, other arithmetic: 3.97 us -> none  [broadcast_by_parts(): jnp.where(lax.axis_index(axis) == root, x, jnp.zeros_like(x))]
    unnamed x21 -> x5, local copies, waits for them, and re-layouts: 5.38 us -> 8.24 us
  transfers between devices with their start and end apart: 6 -> 0, of which waited for: 6 -> 0; matrix products, arithmetic and copies ran while one was open for 1% -> 0% of each run, Pallas kernels for 0% -> 0%
where the time goes in v1:
time: 113 us
  Pallas kernels  104 us (92%)
  local copies, waits for them, and re-layouts  8.24 us (7%)
    pallas_call x1, Pallas kernels, on_device(): pl.pallas_call(kernel, out_shape=(tall, square, tall, square, square), in...  104 us
    unnamed x5, local copies, waits for them, and re-layouts  8.24 us

profile of v1, /device:TPU:1, one launch (start us, length us, event | category | flops | bytes accessed | tf_op | source)
XLA Modules:
  0.0 112.9 jit_solution(11604349226927156415)
XLA Ops:
  0.6 104.1 %selected_inversion.1 = (f32[192,256]{1,0:T(8,128)}, f32[256,256]{1,0:T(8,128)}, f32[192,256]{1,0:T(8,128)}, f32[256,256]{1,0:T(8,128)}, f32[256,256]{1,0:T(8,128)}) custom-call(s32[2,192]{1,0:T(2,128)} %struct.1, f32[3072,1536]{1,0:T(8,128)} %trailing.1, f32[192,256]{1,0:T(8,128)} %first.1, f32[192,256]{1,0:T(8,128)} %second.1, f32[256,256]{1,0:T(8,128)} %link_in.1, ...), custom_call_target="tpu_custom_call" | custom-call | tf_op jit(solution)/shard_map/selected_inversion/pallas_call | solution.py:415
  104.7 1.6 %copy.17 = f32[192,256]{1,0:T(8,128)} copy(f32[192,256]{1,0:T(8,128)} %get-tuple-element.10) | data formatting | bytes 393216
  106.3 1.7 %copy.18 = f32[256,256]{1,0:T(8,128)} copy(f32[256,256]{1,0:T(8,128)} %get-tuple-element.11) | data formatting | bytes 524288
  108.0 1.6 %copy.19 = f32[192,256]{1,0:T(8,128)} copy(f32[192,256]{1,0:T(8,128)} %get-tuple-element.12) | data formatting | bytes 393216
  109.6 1.7 %copy.20 = f32[256,256]{1,0:T(8,128)} copy(f32[256,256]{1,0:T(8,128)} %get-tuple-element.13) | data formatting | bytes 524288
  111.3 1.7 %copy.21 = f32[256,256]{1,0:T(8,128)} copy(f32[256,256]{1,0:T(8,128)} %get-tuple-element.14) | data formatting | bytes 524288

commit v2 on v1

--- a/solution.py
+++ b/solution.py
@@ -1,5 +1,3 @@
-import functools
-
 import jax
 import jax.numpy as jnp
 from jax import lax
@@ -14,14 +12,11 @@
 W = 256
 HALF = 128
 DEPTH = 1536
-SUMS = 3 * W
-PART = SUMS // 32
 
 UNITS = (
-    [(2, 2), (2, 3), (2, 0), (2, 1)]
-    + [(3, 2), (0, 2), (1, 2)]
-    + [(1, 1), (1, 3), (3, 1), (3, 3)]
-    + [(1, 0), (3, 0), (0, 1), (0, 3), (0, 0)]
+    [(2, 2), (2, 3), (3, 2), (2, 1), (1, 2), (2, 0), (0, 2)]
+    + [(1, 1), (1, 3), (3, 1), (1, 0), (0, 1)]
+    + [(3, 3), (3, 0), (0, 3), (0, 0)]
 )
 PLACE = {unit: i for i, unit in enumerate(UNITS)}
 
@@ -60,9 +55,9 @@
     out1, diag1, out2, cross2, diag2,
     t_buf, raw, lead_h, lead_l, prod_a, prod_b, got_a, got_b, far_a, far_b,
     lead, link, inv1, inv2, y_buf,
-    sums, sum_p, sum_q, sum_x, total,
+    sums, sum_p, sum_x, sum_q, total, tail, tail_p, tail_q, tail_x, last,
     t_sem, in_sem, g1_send, g1_recv, g2_send, g2_recv, g3_send, g3_recv,
-    r_send, r_recv, f_send, f_recv, s_send, s_recv,
+    r_send, r_recv, f_send, f_recv, s_send, s_recv, e_send, e_recv,
 ):
     x, k, z, y = (lax.axis_index(name) for name in AXES)
     c = z * 4 + y
@@ -130,7 +125,7 @@
         slot = raw.at[p, lax.rem(z, 2) * 4 + y, pl.ds(q * 48, 48)]
         return pltpu.make_async_copy(panels[p].at[pl.ds(q * 48, 48)], slot, g1_recv.at[p, y])
 
-    for p in range(2):
+    def gather_0(p):
         for q in range(4):
             same = at_home & (x == q)
 
@@ -142,6 +137,7 @@
             def _(p=p, q=q):
                 quarter(p, q).start()
 
+    gather_0(0)
     for copy in own_copies:
         copy.wait()
     for p in range(2):
@@ -264,10 +260,10 @@
                         for h in sends:
                             hop(p, h, UNITS[v]).start()
 
-    def joined(p, h):
-        prod, got, _ = pick(h)
-        for near, far in ((1, 0), (1, 2), (3, 1), (3, 3)):
-            unit = unit_of(h, near, far)
+    def joined(p, far):
+        for h in range(2):
+            prod, got, _ = pick(h)
+            unit = unit_of(h, 1 if far % 2 == 0 else 3, far)
             hop_wait(p, h, 0, far)
             prod[p, PLACE[unit]] = prod[p, PLACE[unit]] + got[p, 0, far]
             hop(p, h, unit).start()
@@ -279,9 +275,9 @@
             f_recv.at[p, h, far - 1], next_to(h, far, phase=2),
         )
 
-    def second_phase(p, h):
-        prod, got, _ = pick(h)
-        for far in (2, 1, 3, 0):
+    def second_phase(p, far):
+        for h in range(2):
+            prod, got, _ = pick(h)
             u = PLACE[unit_of(h, 0, far)]
             hop_wait(p, h, 1, far)
             hop_wait(p, h, 2, far)
@@ -297,94 +293,205 @@
         value = (prod[p, PLACE[(0, 0)]] + got[p, 0]) + (got[p, 1] + got[p, 2])
         y_buf[p, :, pl.ds(h * HALF, HALF)] = value
 
-    def rows_of(core, place):
-        return pl.ds(pl.multiple_of(core * (SUMS // 2) + place * PART, 8), PART)
-
-    def half_of(core):
-        return pl.ds(pl.multiple_of(core * (SUMS // 2), 8), SUMS // 2)
-
-    def reduce_all():
-        swap = remote(sums.at[half_of(1 - k)], sum_p, s_send.at[0], s_recv.at[0], at(dk=1))
-        swap.start()
-        swap.wait_recv()
-        sums[half_of(k)] = sums[half_of(k)] + sum_p[...]
-        for o, (dz, dy) in enumerate(plane):
-            where = at(dz=dz, dy=dy)
-            remote(
-                sums.at[rows_of(k, where[2] * 4 + where[3])], sum_q.at[o], s_send.at[1], s_recv.at[1], where
-            ).start()
-        remote(sum_q, sum_q, s_send.at[1], s_recv.at[1], at(dk=1)).wait_recv()
-        value = sums[rows_of(k, c)]
-        for o in range(15):
-            value = value + sum_q[o]
-        sum_x[x] = value
-        cross = [
-            remote(sum_x.at[x], sum_x.at[x], s_send.at[1 + dx], s_recv.at[1 + dx], at(dx=dx)) for dx in (1, 2, 3)
-        ]
-        for copy in cross:
-            copy.start()
-        for dx in (1, 2, 3):
-            ref = sum_x.at[lax.rem(x - dx + 4, 4)]
-            remote(ref, ref, s_send.at[1 + dx], s_recv.at[1 + dx], at(dx=dx)).wait_recv()
-        mine = rows_of(k, c)
-        total[mine] = (sum_x[0] + sum_x[1]) + (sum_x[2] + sum_x[3])
-        for dz, dy in plane:
-            remote(total.at[mine], total.at[mine], s_send.at[5], s_recv.at[5], at(dz=dz, dy=dy)).start()
-        remote(sum_q, sum_q, s_send.at[5], s_recv.at[5], at(dk=1)).wait_recv()
-        back = remote(total.at[half_of(k)], total.at[half_of(k)], s_send.at[6], s_recv.at[6], at(dk=1))
-        back.start()
-        ref = total.at[half_of(1 - k)]
-        remote(ref, ref, s_send.at[6], s_recv.at[6], at(dk=1)).wait_recv()
-        swap.wait_send()
-        remote(sum_q, sum_q, s_send.at[1], s_recv.at[1], at(dk=1)).wait_send()
-        for copy in cross:
-            copy.wait_send()
-        remote(sum_q, sum_q, s_send.at[5], s_recv.at[5], at(dk=1)).wait_send()
-        back.wait_send()
+    def rows(ref, start, size):
+        return ref.at[pl.ds(pl.multiple_of(start, 8), size)]
+
+    def sent(src, dst, i, where):
+        return remote(src, dst, s_send.at[i], s_recv.at[i], where)
+
+    def spot(ref, start, place):
+        row = pl.multiple_of(start + 8 * lax.div(place, 2), 8)
+        return ref.at[pl.ds(row, 8), pl.ds(pl.multiple_of(lax.rem(place, 2) * HALF, HALF), HALF)]
+
+    quart = k * W + x * 64
+
+    def early_swap(core):
+        return sent(rows(sums, core * W, W), sum_p, 0, at(dk=1))
+
+    def early_x(dx):
+        there = lax.rem(x + dx, 4)
+        return sent(rows(sums, k * W + there * 64, 64), sum_x.at[dx - 1], dx, at(dx=dx))
+
+    def early_plane(o):
+        dz, dy = plane[o]
+        where = at(dz=dz, dy=dy)
+        return sent(spot(sums, quart, where[2] * 4 + where[3]), sum_q.at[o], 4, where)
+
+    def early_spread(o):
+        dz, dy = plane[o]
+        mine = spot(total, quart, c)
+        return sent(mine, mine, 5, at(dz=dz, dy=dy))
+
+    def early_spread_x(dx):
+        mine = rows(total, quart, 64)
+        return sent(mine, mine, 5 + dx, at(dx=dx))
+
+    def early_back(core):
+        half = rows(total, core * W, W)
+        return sent(half, half, 9, at(dk=1))
+
+    def early(step):
+        if step == 0:
+            early_swap(1 - k).start()
+        if step == 1:
+            early_swap(1 - k).wait_recv()
+            half = rows(sums, k * W, W)
+            half[...] = half[...] + sum_p[...]
+            for dx in (2, 1, 3):
+                early_x(dx).start()
+        if step == 2:
+            for dx in (1, 2, 3):
+                early_x(dx).wait_recv()
+            mine = rows(sums, quart, 64)
+            mine[...] = (mine[...] + sum_x[0]) + (sum_x[1] + sum_x[2])
+            for o in range(15):
+                early_plane(o).start()
+        if step == 3:
+            sent(sum_q, sum_q, 4, at(dk=1)).wait_recv()
+            value = spot(sums, quart, c)[...]
+            for o in range(15):
+                value = value + sum_q[o]
+            spot(total, quart, c)[...] = value
+            for o in range(15):
+                early_spread(o).start()
+        if step == 4:
+            sent(sum_q, sum_q, 5, at(dk=1)).wait_recv()
+            for dx in (2, 1, 3):
+                early_spread_x(dx).start()
+        if step == 5:
+            for dx in (1, 2, 3):
+                ref = rows(total, k * W + lax.rem(x - dx + 4, 4) * 64, 64)
+                sent(ref, ref, 5 + dx, at(dx=dx)).wait_recv()
+            early_back(k).start()
+        if step == 6:
+            early_back(1 - k).wait_recv()
+
+    def late_sent(src, dst, i, where):
+        return remote(src, dst, e_send.at[i], e_recv.at[i], where)
+
+    def late_swap(core):
+        return late_sent(rows(tail, core * HALF, HALF), tail_p, 0, at(dk=1))
+
+    def late_plane(o):
+        dz, dy = plane[o]
+        where = at(dz=dz, dy=dy)
+        return late_sent(rows(tail, k * HALF + 8 * (where[2] * 4 + where[3]), 8), tail_q.at[o], 1, where)
+
+    def late_x(dx):
+        return late_sent(tail_x.at[x], tail_x.at[x], 1 + dx, at(dx=dx))
+
+    def late_spread(o):
+        dz, dy = plane[o]
+        mine = rows(last, k * HALF + 8 * c, 8)
+        return late_sent(mine, mine, 5, at(dz=dz, dy=dy))
+
+    def late_back(core):
+        half = rows(last, core * HALF, HALF)
+        return late_sent(half, half, 6, at(dk=1))
+
+    def late(step):
+        if step == 0:
+            late_swap(1 - k).start()
+        if step == 1:
+            late_swap(1 - k).wait_recv()
+            half = rows(tail, k * HALF, HALF)
+            half[...] = half[...] + tail_p[...]
+            for o in range(15):
+                late_plane(o).start()
+        if step == 2:
+            late_sent(tail_q, tail_q, 1, at(dk=1)).wait_recv()
+            value = rows(tail, k * HALF + 8 * c, 8)[...]
+            for o in range(15):
+                value = value + tail_q[o]
+            tail_x[x] = value
+            for dx in (2, 1, 3):
+                late_x(dx).start()
+        if step == 3:
+            for dx in (1, 2, 3):
+                ref = tail_x.at[lax.rem(x - dx + 4, 4)]
+                late_sent(ref, ref, 1 + dx, at(dx=dx)).wait_recv()
+            rows(last, k * HALF + 8 * c, 8)[...] = (tail_x[0] + tail_x[1]) + (tail_x[2] + tail_x[3])
+            for o in range(15):
+                late_spread(o).start()
+        if step == 4:
+            late_sent(tail_q, tail_q, 5, at(dk=1)).wait_recv()
+            late_back(k).start()
+        if step == 5:
+            late_back(1 - k).wait_recv()
 
     gather_1(0)
     gather_2(0)
     gather_3(0)
     gather_4(0)
+    gather_0(1)
     gather_5(0)
-    compute(0, 0, 4)
+    compute(0, 0, 7)
+    compute(0, 7, 12)
     gather_1(1)
-    compute(0, 4, 7)
+    joined(0, 2)
+    joined(0, 1)
+    compute(0, 12, 16)
     gather_2(1)
-    compute(0, 7, 11)
+    joined(0, 3)
+    joined(0, 0)
     gather_3(1)
     gather_4(1)
-    compute(0, 11, 16)
-    joined(0, 0)
-    joined(0, 1)
+    second_phase(0, 2)
     gather_5(1)
-    compute(1, 0, 4)
-    compute(1, 4, 7)
+    compute(1, 0, 7)
+    second_phase(0, 1)
+    compute(1, 7, 12)
+    second_phase(0, 3)
+    joined(1, 2)
+    joined(1, 1)
+    compute(1, 12, 16)
     second_phase(0, 0)
-    compute(1, 7, 11)
-    second_phase(0, 1)
-    compute(1, 11, 16)
+    joined(1, 3)
     joined(1, 0)
-    joined(1, 1)
     finish(0, 0)
     finish(0, 1)
+    for p in range(2):
+        sums[pl.ds(p * W, W)] = exact(lead[p], y_buf[0], (0, 0))
+    early(0)
     out1[...] = -y_buf[0]
     out2[...] = exact(y_buf[0], link[...])
-    for p in range(2):
-        sums[pl.ds(p * W, W)] = exact(lead[p], y_buf[0], (0, 0))
+    second_phase(1, 2)
+    early(1)
+    second_phase(1, 1)
+    early(2)
+    second_phase(1, 3)
+    early(3)
     second_phase(1, 0)
-    second_phase(1, 1)
     finish(1, 0)
     finish(1, 1)
+    tail[...] = exact(lead[1], y_buf[1], (0, 0))
+    late(0)
+    early(4)
+    late(1)
     out2[...] = out2[...] - y_buf[1]
-    sums[pl.ds(2 * W, W)] = exact(lead[1], y_buf[1], (0, 0))
-    reduce_all()
+    early(5)
+    late(2)
+    early(6)
     diag1[...] = inv1[...] + total[pl.ds(0, W)]
     cross2[...] = jnp.transpose(total[pl.ds(W, W)]) - exact(diag1[...], link[...])
-    diag2[...] = (
-        (inv2[...] - exact(link[...], cross2[...], (0, 0))) - exact(total[pl.ds(W, W)], link[...])
-    ) + total[pl.ds(2 * W, W)]
-
+    late(3)
+    diag2[...] = (inv2[...] - exact(link[...], cross2[...], (0, 0))) - exact(total[pl.ds(W, W)], link[...])
+    late(4)
+    late(5)
+    diag2[...] = diag2[...] + last[...]
+
+    early_swap(1 - k).wait_send()
+    late_swap(1 - k).wait_send()
+    for dx in (1, 2, 3):
+        early_x(dx).wait_send()
+        early_spread_x(dx).wait_send()
+        late_x(dx).wait_send()
+    for i in (4, 5):
+        sent(sum_q, sum_q, i, at(dk=1)).wait_send()
+    for i in (1, 5):
+        late_sent(tail_q, tail_q, i, at(dk=1)).wait_send()
+    early_back(k).wait_send()
+    late_back(k).wait_send()
     for p in range(2):
         for q in range(4):
 
@@ -405,6 +512,11 @@
                 second_send(p, h, far).wait_send()
 
 
+def write_out(*refs):
+    for src, dst in zip(refs[:5], refs[5:]):
+        dst[...] = src[...]
+
+
 def on_device(trailing, first, second, link, inv1, inv2, struct):
     f32, bf16 = jnp.float32, jnp.bfloat16
     square = jax.ShapeDtypeStruct((W, W), f32)
@@ -412,7 +524,7 @@
     vmem, anywhere = pl.BlockSpec(memory_space=pltpu.VMEM), pl.BlockSpec(memory_space=pl.ANY)
     dma = pltpu.SemaphoreType.DMA
     block = (ROWS, HALF)
-    return pl.pallas_call(
+    parts = pl.pallas_call(
         kernel,
         out_shape=(tall, square, tall, square, square),
         in_specs=[pl.BlockSpec(memory_space=pltpu.SMEM)] + [anywhere] * 6,
@@ -433,19 +545,28 @@
             pltpu.VMEM((W, W), f32),
             pltpu.VMEM((W, W), f32),
             pltpu.VMEM((2, ROWS, W), f32),
-            pltpu.VMEM((SUMS, W), f32),
-            pltpu.VMEM((SUMS // 2, W), f32),
-            pltpu.VMEM((15, PART, W), f32),
-            pltpu.VMEM((4, PART, W), f32),
-            pltpu.VMEM((SUMS, W), f32),
+            pltpu.VMEM((2 * W, W), f32),
+            pltpu.VMEM((W, W), f32),
+            pltpu.VMEM((3, 64, W), f32),
+            pltpu.VMEM((15, 8, HALF), f32),
+            pltpu.VMEM((2 * W, W), f32),
+            pltpu.VMEM((W, W), f32),
+            pltpu.VMEM((HALF, W), f32),
+            pltpu.VMEM((15, 8, W), f32),
+            pltpu.VMEM((4, 8, W), f32),
+            pltpu.VMEM((W, W), f32),
             dma((16,)), dma((5,)), dma((2, 4)), dma((2, 4)), dma((2, 2, 3)), dma((2, 2, 3)), dma((2, 4)), dma((2, 4)),
-            dma((2, 2, 3, 4)), dma((2, 2, 3, 4)), dma((2, 2, 3)), dma((2, 2, 3)), dma((7,)), dma((7,)),
+            dma((2, 2, 3, 4)), dma((2, 2, 3, 4)), dma((2, 2, 3)), dma((2, 2, 3)), dma((10,)), dma((10,)), dma((7,)), dma((7,)),
         ],
         compiler_params=pltpu.CompilerParams(
             collective_id=0, has_side_effects=True, vmem_limit_bytes=60 * 1024 * 1024
         ),
         name="selected_inversion",
     )(struct, trailing, first, second, link, inv1, inv2)
+    return pl.pallas_call(
+        write_out, out_shape=(tall, square, tall, square, square), in_specs=[vmem] * 5, out_specs=(vmem,) * 5,
+        name="write_out",
+    )(*parts)
 
 
 def solution(mesh):

time: 113 us -> 102 us (0.903)
  local copies, waits for them, and re-layouts: 8.24 us -> 0 us
  Pallas kernels: 104 us -> 101 us
    unnamed x5 -> x0, local copies, waits for them, and re-layouts: 8.24 us -> none
    pallas_call x1, Pallas kernels: 104 us -> 99.1 us  [on_device(): pl.pallas_call(kernel, out_shape=(tall, square, tall, square, square), in...]
    pallas_call x0 -> x1, Pallas kernels: none -> 2.25 us  [on_device(): pl.pallas_call(write_out, out_shape=(tall, square, tall, square, square),...]
where the time goes in v2:
time: 102 us
  Pallas kernels  101 us (99%)
    pallas_call x1, Pallas kernels, on_device(): pl.pallas_call(kernel, out_shape=(tall, square, tall, square, square), in...  99.1 us
    pallas_call x1, Pallas kernels, on_device(): pl.pallas_call(write_out, out_shape=(tall, square, tall, square, square),...  2.25 us

profile of v2, /device:TPU:1, one launch (start us, length us, event | category | flops | bytes accessed | tf_op | source)
XLA Modules:
  0.0 102.0 jit_solution(15843663692845120743)
XLA Ops:
  0.6 99.1 %selected_inversion.1 = (f32[192,256]{1,0:T(8,128)}, f32[256,256]{1,0:T(8,128)}, f32[192,256]{1,0:T(8,128)}, f32[256,256]{1,0:T(8,128)}, f32[256,256]{1,0:T(8,128)}) custom-call(s32[2,192]{1,0:T(2,128)} %struct.1, f32[3072,1536]{1,0:T(8,128)} %trailing.1, f32[192,256]{1,0:T(8,128)} %first.1, f32[192,256]{1,0:T(8,128)} %second.1, f32[256,256]{1,0:T(8,128)} %link_in.1, ...), custom_call_target="tpu_custom_call" | custom-call | tf_op jit(solution)/shard_map/selected_inversion/pallas_call | solution.py:527
  99.7 2.3 %write_out.1 = (f32[192,256]{1,0:T(8,128)}, f32[256,256]{1,0:T(8,128)}, f32[192,256]{1,0:T(8,128)}, f32[256,256]{1,0:T(8,128)}, f32[256,256]{1,0:T(8,128)}) custom-call(f32[192,256]{1,0:T(8,128)} %get-tuple-element.10.refs_0_, f32[256,256]{1,0:T(8,128)} %get-tuple-element.11.refs_1_, f32[192,256]{1,0:T(8,128)} %get-tuple-element.12.refs_2_, ...), custom_call_target="tpu_custom_call" | custom-call | tf_op jit(solution)/shard_map/write_out/pallas_call | solution.py:566

commit v3 on v2

--- a/solution.py
+++ b/solution.py
@@ -15,8 +15,8 @@
 
 UNITS = (
     [(2, 2), (2, 3), (3, 2), (2, 1), (1, 2), (2, 0), (0, 2)]
-    + [(1, 1), (1, 3), (3, 1), (1, 0), (0, 1)]
-    + [(3, 3), (3, 0), (0, 3), (0, 0)]
+    + [(1, 3), (3, 1), (3, 3), (1, 0), (0, 1)]
+    + [(1, 1), (3, 0), (0, 3), (0, 0)]
 )
 PLACE = {unit: i for i, unit in enumerate(UNITS)}
 
@@ -55,9 +55,9 @@
     out1, diag1, out2, cross2, diag2,
     t_buf, raw, lead_h, lead_l, prod_a, prod_b, got_a, got_b, far_a, far_b,
     lead, link, inv1, inv2, y_buf,
-    sums, sum_p, sum_x, sum_q, total, tail, tail_p, tail_q, tail_x, last,
+    sums, sum_p, sum_x, sum_q, total, tail, tail_p, tail_q, tail_x, last, tall, square,
     t_sem, in_sem, g1_send, g1_recv, g2_send, g2_recv, g3_send, g3_recv,
-    r_send, r_recv, f_send, f_recv, s_send, s_recv, e_send, e_recv,
+    r_send, r_recv, f_send, f_recv, s_send, s_recv, e_send, e_recv, out_sem,
 ):
     x, k, z, y = (lax.axis_index(name) for name in AXES)
     c = z * 4 + y
@@ -119,7 +119,7 @@
 
     def quarter(p, q):
         slot = raw.at[p, lax.rem(z, 2) * 4 + y, pl.ds(q * 48, 48)]
-        return remote(panels[p].at[pl.ds(q * 48, 48)], slot, g1_send.at[p, q], g1_recv.at[p, y], target[q])
+        return remote(panels[p].at[pl.ds(q * 48, 48)], slot, g1_send.at[p], g1_recv.at[p, y], target[q])
 
     def quarter_home(p, q):
         slot = raw.at[p, lax.rem(z, 2) * 4 + y, pl.ds(q * 48, 48)]
@@ -146,58 +146,56 @@
             mask = struct[p, lax.div(flat * 3 + s, 2)].astype(jnp.float32)
             lead[p, rows] = lead[p, rows] * mask
 
-    def pieces(p, lo, n, dx):
-        q = lax.rem(x + dx + 4, 4)
-        return raw.at[p, pl.ds(4 * k + lo, n), pl.ds(pl.multiple_of(q * 48, 48), 48)]
+    def piece(p, d, dx):
+        q, i = lax.rem(x + dx + 4, 4), lax.rem(y + d, 4)
+        return raw.at[p, 4 * k + i, pl.ds(pl.multiple_of(q * 48, 48), 48)]
+
+    passed = ((0, 3), (1, 2))
 
     def ring(p, way, m):
         step = 1 if way == 0 else -1
-        lo = (0, 2, 0)[m] if way == 0 else (2, 0, 2)[m]
-        ref = pieces(p, lo, 2, -step if m == 2 else 0)
-        return remote(ref, ref, g2_send.at[p, way, m], g2_recv.at[p, way, m], at(dx=step))
+        ref = piece(p, m, 0) if m < 4 else piece(p, passed[way][m - 4], -step)
+        return remote(ref, ref, g2_send.at[p], g2_recv.at[p, way, m], at(dx=step))
 
     def ring_wait(p, way, m):
         step = 1 if way == 0 else -1
-        lo = (0, 2, 0)[m] if way == 0 else (2, 0, 2)[m]
-        ref = pieces(p, lo, 2, -2 * step if m == 2 else -step)
-        remote(ref, ref, g2_send.at[p, way, m], g2_recv.at[p, way, m], at(dx=step)).wait_recv()
+        ref = piece(p, m, -step) if m < 4 else piece(p, passed[way][m - 4], -2 * step)
+        remote(ref, ref, g2_send.at[p], g2_recv.at[p, way, m], at(dx=step)).wait_recv()
 
     def across(p, m):
-        ref = pieces(p, 0, 4, (0, -1, 1, 2)[m])
-        return remote(ref, ref, g3_send.at[p, m], g3_recv.at[p, m], at(dk=1))
-
-    def across_wait(p, m):
         q = lax.rem(x + (0, -1, 1, 2)[m] + 4, 4)
-        ref = raw.at[p, pl.ds(4 * (1 - k), 4), pl.ds(pl.multiple_of(q * 48, 48), 48)]
-        remote(ref, ref, g3_send.at[p, m], g3_recv.at[p, m], at(dk=1)).wait_recv()
+        ref = raw.at[p, pl.ds(4 * k, 4), pl.ds(pl.multiple_of(q * 48, 48), 48)]
+        return remote(ref, ref, g3_send.at[p], g3_recv.at[p], at(dk=1))
 
     def gather_1(p):
-        for i in range(4):
-            ref = raw.at[p, 4 * k + i, pl.ds(pl.multiple_of(x * 48, 48), 48)]
-            pltpu.make_async_copy(ref, ref, g1_recv.at[p, i]).wait()
+        for d in (0, 1, 3, 2):
+            ref = piece(p, d, 0)
+            pltpu.make_async_copy(ref, ref, g1_recv.at[p, lax.rem(y + d, 4)]).wait()
+            for way in range(2):
+                ring(p, way, d).start()
+        across(p, 0).start()
+
+    def gather_2(p):
         for m in range(2):
             for way in range(2):
-                ring(p, way, m).start()
-        across(p, 0).start()
-
-    def gather_2(p):
-        for way in range(2):
-            ring_wait(p, way, 0)
-            ring(p, way, 2).start()
+                ring_wait(p, way, passed[way][m])
+                ring(p, way, 4 + m).start()
 
     def gather_3(p):
         for way in range(2):
-            ring_wait(p, way, 1)
+            for d in passed[1 - way]:
+                ring_wait(p, way, d)
             across(p, 1 + way).start()
 
     def gather_4(p):
         for way in range(2):
-            ring_wait(p, way, 2)
+            for m in (4, 5):
+                ring_wait(p, way, m)
         across(p, 3).start()
 
     def gather_5(p):
-        for m in range(4):
-            across_wait(p, m)
+        ref = raw.at[p, pl.ds(4 * (1 - k), 4)]
+        remote(ref, ref, g3_send.at[p], g3_recv.at[p], at(dk=1)).wait_recv()
 
         @pl.loop(0, 8)
         def _(j):
@@ -225,14 +223,14 @@
         prod, got, _ = pick(h)
         slot = 0 if kind == "relay" else (1 if way == 1 else 2)
         return remote(
-            prod.at[p, PLACE[unit]], got.at[p, slot, far], r_send.at[p, h, slot, far], r_recv.at[p, h, slot, far],
+            prod.at[p, PLACE[unit]], got.at[p, slot, far], r_send.at[p, h], r_recv.at[p, h, slot, far],
             next_to(h, way),
         )
 
     def hop_wait(p, h, slot, far):
         _, got, _ = pick(h)
         ref = got.at[p, slot, far]
-        remote(ref, ref, r_send.at[p, h, slot, far], r_recv.at[p, h, slot, far], next_to(h, 1)).wait_recv()
+        remote(ref, ref, r_send.at[p, h], r_recv.at[p, h, slot, far], next_to(h, 1)).wait_recv()
 
     def unit_of(h, near, far):
         return (near, far) if h == 0 else (far, near)
@@ -268,29 +266,42 @@
             prod[p, PLACE[unit]] = prod[p, PLACE[unit]] + got[p, 0, far]
             hop(p, h, unit).start()
 
-    def second_send(p, h, far):
+    def second_send(p, h, m):
         prod, _, got = pick(h)
+        far, way, lo, n = ((2, 1, 0, 96), (2, -1, 96, 96), (1, 1, 0, ROWS), (3, -1, 0, ROWS))[m]
+        part = pl.ds(lo, n)
         return remote(
-            prod.at[p, PLACE[unit_of(h, 0, far)]], got.at[p, far - 1], f_send.at[p, h, far - 1],
-            f_recv.at[p, h, far - 1], next_to(h, far, phase=2),
+            prod.at[p, PLACE[unit_of(h, 0, far)], part], got.at[p, max(0, m - 1), part], f_send.at[p, h],
+            f_recv.at[p, h, m], next_to(h, way, phase=2),
         )
+
+    def second_wait(p, h, m):
+        _, _, got = pick(h)
+        ref = got.at[p, max(0, m - 1), pl.ds(96 if m == 1 else 0, 96 if m < 2 else ROWS)]
+        remote(ref, ref, f_send.at[p, h], f_recv.at[p, h, m], next_to(h, 1, phase=2)).wait_recv()
 
     def second_phase(p, far):
         for h in range(2):
-            prod, got, _ = pick(h)
+            prod, got, last_got = pick(h)
             u = PLACE[unit_of(h, 0, far)]
             hop_wait(p, h, 1, far)
             hop_wait(p, h, 2, far)
             prod[p, u] = prod[p, u] + (got[p, 1, far] + got[p, 2, far])
-            if far:
-                second_send(p, h, far).start()
+            if far == 2:
+                second_send(p, h, 0).start()
+                second_send(p, h, 1).start()
+            if far in (1, 3):
+                m = far // 2
+                second_wait(p, h, m)
+                part = pl.ds(96 * m, 96)
+                prod[p, u, part] = prod[p, u, part] + last_got[p, 0, part]
+                second_send(p, h, 2 + m).start()
 
     def finish(p, h):
         prod, _, got = pick(h)
-        for far in (1, 2, 3):
-            ref = got.at[p, far - 1]
-            remote(ref, ref, f_send.at[p, h, far - 1], f_recv.at[p, h, far - 1], next_to(h, far, 2)).wait_recv()
-        value = (prod[p, PLACE[(0, 0)]] + got[p, 0]) + (got[p, 1] + got[p, 2])
+        second_wait(p, h, 2)
+        second_wait(p, h, 3)
+        value = prod[p, PLACE[(0, 0)]] + (got[p, 1] + got[p, 2])
         y_buf[p, :, pl.ds(h * HALF, HALF)] = value
 
     def rows(ref, start, size):
@@ -310,25 +321,25 @@
 
     def early_x(dx):
         there = lax.rem(x + dx, 4)
-        return sent(rows(sums, k * W + there * 64, 64), sum_x.at[dx - 1], dx, at(dx=dx))
+        return sent(rows(sums, k * W + there * 64, 64), sum_x.at[dx - 1], 1, at(dx=dx))
 
     def early_plane(o):
         dz, dy = plane[o]
         where = at(dz=dz, dy=dy)
-        return sent(spot(sums, quart, where[2] * 4 + where[3]), sum_q.at[o], 4, where)
+        return sent(spot(sums, quart, where[2] * 4 + where[3]), sum_q.at[o], 2, where)
 
     def early_spread(o):
         dz, dy = plane[o]
         mine = spot(total, quart, c)
-        return sent(mine, mine, 5, at(dz=dz, dy=dy))
+        return sent(mine, mine, 3, at(dz=dz, dy=dy))
 
     def early_spread_x(dx):
         mine = rows(total, quart, 64)
-        return sent(mine, mine, 5 + dx, at(dx=dx))
+        return sent(mine, mine, 4, at(dx=dx))
 
     def early_back(core):
         half = rows(total, core * W, W)
-        return sent(half, half, 9, at(dk=1))
+        return sent(half, half, 5, at(dk=1))
 
     def early(step):
         if step == 0:
@@ -340,14 +351,13 @@
             for dx in (2, 1, 3):
                 early_x(dx).start()
         if step == 2:
-            for dx in (1, 2, 3):
-                early_x(dx).wait_recv()
+            sent(sum_x, sum_x, 1, at(dk=1)).wait_recv()
             mine = rows(sums, quart, 64)
             mine[...] = (mine[...] + sum_x[0]) + (sum_x[1] + sum_x[2])
             for o in range(15):
                 early_plane(o).start()
         if step == 3:
-            sent(sum_q, sum_q, 4, at(dk=1)).wait_recv()
+            sent(sum_q, sum_q, 2, at(dk=1)).wait_recv()
             value = spot(sums, quart, c)[...]
             for o in range(15):
                 value = value + sum_q[o]
@@ -355,13 +365,11 @@
             for o in range(15):
                 early_spread(o).start()
         if step == 4:
-            sent(sum_q, sum_q, 5, at(dk=1)).wait_recv()
+            sent(sum_q, sum_q, 3, at(dk=1)).wait_recv()
             for dx in (2, 1, 3):
                 early_spread_x(dx).start()
         if step == 5:
-            for dx in (1, 2, 3):
-                ref = rows(total, k * W + lax.rem(x - dx + 4, 4) * 64, 64)
-                sent(ref, ref, 5 + dx, at(dx=dx)).wait_recv()
+            sent(sum_x, sum_x, 4, at(dk=1)).wait_recv()
             early_back(k).start()
         if step == 6:
             early_back(1 - k).wait_recv()
@@ -378,16 +386,20 @@
         return late_sent(rows(tail, k * HALF + 8 * (where[2] * 4 + where[3]), 8), tail_q.at[o], 1, where)
 
     def late_x(dx):
-        return late_sent(tail_x.at[x], tail_x.at[x], 1 + dx, at(dx=dx))
+        return late_sent(tail_x.at[x], tail_x.at[x], 2, at(dx=dx))
 
     def late_spread(o):
         dz, dy = plane[o]
         mine = rows(last, k * HALF + 8 * c, 8)
-        return late_sent(mine, mine, 5, at(dz=dz, dy=dy))
+        return late_sent(mine, mine, 3, at(dz=dz, dy=dy))
 
     def late_back(core):
         half = rows(last, core * HALF, HALF)
-        return late_sent(half, half, 6, at(dk=1))
+        return late_sent(half, half, 4, at(dk=1))
+
+    def tail_half(core):
+        side = lead[1, :, pl.ds(pl.multiple_of(core * HALF, HALF), HALF)]
+        rows(tail, core * HALF, HALF)[...] = exact(side, y_buf[1], (0, 0))
 
     def late(step):
         if step == 0:
@@ -407,128 +419,144 @@
             for dx in (2, 1, 3):
                 late_x(dx).start()
         if step == 3:
-            for dx in (1, 2, 3):
-                ref = tail_x.at[lax.rem(x - dx + 4, 4)]
-                late_sent(ref, ref, 1 + dx, at(dx=dx)).wait_recv()
+            three = tail_x.at[pl.ds(0, 3)]
+            late_sent(three, three, 2, at(dx=1)).wait_recv()
             rows(last, k * HALF + 8 * c, 8)[...] = (tail_x[0] + tail_x[1]) + (tail_x[2] + tail_x[3])
             for o in range(15):
                 late_spread(o).start()
         if step == 4:
-            late_sent(tail_q, tail_q, 5, at(dk=1)).wait_recv()
+            late_sent(tail_q, tail_q, 3, at(dk=1)).wait_recv()
             late_back(k).start()
         if step == 5:
             late_back(1 - k).wait_recv()
 
+    def out_copy(i):
+        src = (tall.at[0], square.at[0], tall.at[1], square.at[1], square.at[2])[i]
+        dst = (out1, diag1, out2, cross2, diag2)[i]
+        return pltpu.make_async_copy(src, dst, out_sem.at[i])
+
     gather_1(0)
     gather_2(0)
+    gather_0(1)
     gather_3(0)
     gather_4(0)
-    gather_0(1)
     gather_5(0)
-    compute(0, 0, 7)
+    compute(0, 0, 4)
+    gather_1(1)
+    compute(0, 4, 7)
     compute(0, 7, 12)
-    gather_1(1)
     joined(0, 2)
+    gather_2(1)
+    compute(0, 12, 16)
+    joined(0, 3)
     joined(0, 1)
-    compute(0, 12, 16)
-    gather_2(1)
-    joined(0, 3)
     joined(0, 0)
     gather_3(1)
     gather_4(1)
+    gather_5(1)
+    compute(1, 0, 4)
     second_phase(0, 2)
-    gather_5(1)
-    compute(1, 0, 7)
+    compute(1, 4, 7)
+    compute(1, 7, 12)
+    joined(1, 2)
+    compute(1, 12, 16)
+    joined(1, 3)
+    second_phase(0, 3)
     second_phase(0, 1)
-    compute(1, 7, 12)
-    second_phase(0, 3)
-    joined(1, 2)
+    second_phase(0, 0)
     joined(1, 1)
-    compute(1, 12, 16)
-    second_phase(0, 0)
-    joined(1, 3)
     joined(1, 0)
+    second_phase(1, 2)
     finish(0, 0)
     finish(0, 1)
     for p in range(2):
         sums[pl.ds(p * W, W)] = exact(lead[p], y_buf[0], (0, 0))
     early(0)
-    out1[...] = -y_buf[0]
-    out2[...] = exact(y_buf[0], link[...])
-    second_phase(1, 2)
+    tall[0] = -y_buf[0]
+    out_copy(0).start()
     early(1)
+    second_phase(1, 3)
     second_phase(1, 1)
+    tall[1] = exact(y_buf[0], link[...])
+    second_phase(1, 0)
     early(2)
-    second_phase(1, 3)
-    early(3)
-    second_phase(1, 0)
     finish(1, 0)
     finish(1, 1)
-    tail[...] = exact(lead[1], y_buf[1], (0, 0))
+    tail_half(1 - k)
     late(0)
+    tail_half(k)
+    tall[1] = tall[1] - y_buf[1]
+    out_copy(2).start()
+    late(1)
+    early(3)
+    late(2)
     early(4)
-    late(1)
-    out2[...] = out2[...] - y_buf[1]
+    late(3)
     early(5)
-    late(2)
     early(6)
-    diag1[...] = inv1[...] + total[pl.ds(0, W)]
-    cross2[...] = jnp.transpose(total[pl.ds(W, W)]) - exact(diag1[...], link[...])
-    late(3)
-    diag2[...] = (inv2[...] - exact(link[...], cross2[...], (0, 0))) - exact(total[pl.ds(W, W)], link[...])
+    square[0] = inv1[...] + total[pl.ds(0, W)]
+    out_copy(1).start()
+    square[1] = jnp.transpose(total[pl.ds(W, W)]) - exact(square[0], link[...])
+    out_copy(3).start()
+    square[2] = (inv2[...] - exact(link[...], square[1], (0, 0))) - exact(total[pl.ds(W, W)], link[...])
+    for p in range(2):
+
+        @pl.when(at_home)
+        def _(p=p):
+            three = raw.at[p, 0, pl.ds(0, 144)]
+            remote(three, three, g1_send.at[p], g1_recv.at[p, 0], at(dk=1)).wait_send()
+
+        @pl.when(jnp.logical_not(at_home))
+        def _(p=p):
+            remote(raw.at[p, 0], raw.at[p, 0], g1_send.at[p], g1_recv.at[p, 0], at(dk=1)).wait_send()
+
+        twelve, sixteen = raw.at[p, pl.ds(0, 3)], raw.at[p, pl.ds(0, 4)]
+        remote(twelve, twelve, g2_send.at[p], g2_recv.at[p, 0, 0], at(dk=1)).wait_send()
+        remote(sixteen, sixteen, g3_send.at[p], g3_recv.at[p], at(dk=1)).wait_send()
+        for h in range(2):
+            _, got, final = pick(h)
+            remote(got.at[p], got.at[p], r_send.at[p, h], r_recv.at[p, h, 0, 0], at(dk=1)).wait_send()
+            remote(final.at[p], final.at[p], f_send.at[p, h], f_recv.at[p, h, 0], at(dk=1)).wait_send()
+    for ref, i in ((sum_p, 0), (sum_x, 1), (sum_q, 2), (sum_q, 3), (sum_x, 4), (sum_p, 5)):
+        sent(ref, ref, i, at(dk=1)).wait_send()
+    for ref, i in ((tail_p, 0), (tail_q, 1), (tail_x.at[pl.ds(0, 3)], 2)):
+        late_sent(ref, ref, i, at(dk=1)).wait_send()
+    for i in range(4):
+        out_copy(i).wait()
     late(4)
     late(5)
-    diag2[...] = diag2[...] + last[...]
-
-    early_swap(1 - k).wait_send()
-    late_swap(1 - k).wait_send()
-    for dx in (1, 2, 3):
-        early_x(dx).wait_send()
-        early_spread_x(dx).wait_send()
-        late_x(dx).wait_send()
-    for i in (4, 5):
-        sent(sum_q, sum_q, i, at(dk=1)).wait_send()
-    for i in (1, 5):
-        late_sent(tail_q, tail_q, i, at(dk=1)).wait_send()
-    early_back(k).wait_send()
+    square[2] = square[2] + last[...]
+    out_copy(4).start()
+    late_sent(tail_q, tail_q, 3, at(dk=1)).wait_send()
     late_back(k).wait_send()
-    for p in range(2):
-        for q in range(4):
-
-            @pl.when(jnp.logical_not(at_home & (x == q)))
-            def _(p=p, q=q):
-                quarter(p, q).wait_send()
-
-        for way in range(2):
-            for m in range(3):
-                ring(p, way, m).wait_send()
-        for m in range(4):
-            across(p, m).wait_send()
-        for h in range(2):
-            for unit in UNITS:
-                if roles(h, unit)[2] != "keep":
-                    hop(p, h, unit).wait_send()
-            for far in (1, 2, 3):
-                second_send(p, h, far).wait_send()
+    out_copy(4).wait()
 
 
 def write_out(*refs):
-    for src, dst in zip(refs[:5], refs[5:]):
-        dst[...] = src[...]
+    sources, results, held, sems = refs[:5], refs[5:10], refs[10:15], refs[15]
+    into = [pltpu.make_async_copy(a, b, sems.at[0, i]) for i, (a, b) in enumerate(zip(sources, held))]
+    out = [pltpu.make_async_copy(a, b, sems.at[1, i]) for i, (a, b) in enumerate(zip(held, results))]
+    for copy in into:
+        copy.start()
+    for first, second in zip(into, out):
+        first.wait()
+        second.start()
+    for copy in out:
+        copy.wait()
 
 
 def on_device(trailing, first, second, link, inv1, inv2, struct):
     f32, bf16 = jnp.float32, jnp.bfloat16
     square = jax.ShapeDtypeStruct((W, W), f32)
     tall = jax.ShapeDtypeStruct((ROWS, W), f32)
-    vmem, anywhere = pl.BlockSpec(memory_space=pltpu.VMEM), pl.BlockSpec(memory_space=pl.ANY)
+    anywhere = pl.BlockSpec(memory_space=pl.ANY)
     dma = pltpu.SemaphoreType.DMA
     block = (ROWS, HALF)
     parts = pl.pallas_call(
         kernel,
         out_shape=(tall, square, tall, square, square),
         in_specs=[pl.BlockSpec(memory_space=pltpu.SMEM)] + [anywhere] * 6,
-        out_specs=(vmem,) * 5,
+        out_specs=(anywhere,) * 5,
         scratch_shapes=[
             pltpu.VMEM((16, ROWS, DEPTH), f32),
             pltpu.VMEM((2, 8, ROWS, W), f32),
@@ -555,8 +583,11 @@
             pltpu.VMEM((15, 8, W), f32),
             pltpu.VMEM((4, 8, W), f32),
             pltpu.VMEM((W, W), f32),
-            dma((16,)), dma((5,)), dma((2, 4)), dma((2, 4)), dma((2, 2, 3)), dma((2, 2, 3)), dma((2, 4)), dma((2, 4)),
-            dma((2, 2, 3, 4)), dma((2, 2, 3, 4)), dma((2, 2, 3)), dma((2, 2, 3)), dma((10,)), dma((10,)), dma((7,)), dma((7,)),
+            pltpu.VMEM((2, ROWS, W), f32),
+            pltpu.VMEM((3, W, W), f32),
+            dma((16,)), dma((5,)), dma((2,)), dma((2, 4)), dma((2,)), dma((2, 2, 6)), dma((2,)), dma((2,)),
+            dma((2, 2)), dma((2, 2, 3, 4)), dma((2, 2)), dma((2, 2, 4)), dma((6,)), dma((6,)), dma((5,)), dma((5,)),
+            dma((5,)),
         ],
         compiler_params=pltpu.CompilerParams(
             collective_id=0, has_side_effects=True, vmem_limit_bytes=60 * 1024 * 1024
@@ -564,7 +595,12 @@
         name="selected_inversion",
     )(struct, trailing, first, second, link, inv1, inv2)
     return pl.pallas_call(
-        write_out, out_shape=(tall, square, tall, square, square), in_specs=[vmem] * 5, out_specs=(vmem,) * 5,
+        write_out,
+        out_shape=(tall, square, tall, square, square),
+        in_specs=[anywhere] * 5,
+        out_specs=(anywhere,) * 5,
+        scratch_shapes=[pltpu.VMEM(a.shape, f32) for a in (tall, square, tall, square, square)] + [dma((2, 5))],
+        compiler_params=pltpu.CompilerParams(vmem_limit_bytes=60 * 1024 * 1024),
         name="write_out",
     )(*parts)
 

time: 102 us -> 91.5 us (0.90)
  Pallas kernels: 101 us -> 90.6 us
    pallas_call x1, Pallas kernels: 99.1 us -> 88.5 us  [on_device(): pl.pallas_call(kernel, out_shape=(tall, square, tall, square, square), in...]
where the time goes in v3:
time: 91.5 us; the launch traced here: 91.2 us
  Pallas kernels  90.6 us (99%)
    pallas_call x1, Pallas kernels, on_device(): pl.pallas_call(kernel, out_shape=(tall, square, tall, square, square), in...  88.5 us
    pallas_call x1, Pallas kernels, on_device(): pl.pallas_call(write_out, out_shape=(tall, square, tall, square, square),...  2.1 us

profile of v3, /device:TPU:1, one launch (start us, length us, event | category | flops | bytes accessed | tf_op | source)
XLA Modules:
  0.0 91.2 jit_solution(12448370136283498991)
XLA Ops:
  0.6 88.5 %selected_inversion.1 = (f32[192,256]{1,0:T(8,128)}, f32[256,256]{1,0:T(8,128)}, f32[192,256]{1,0:T(8,128)}, f32[256,256]{1,0:T(8,128)}, f32[256,256]{1,0:T(8,128)}) custom-call(s32[2,192]{1,0:T(2,128)} %struct.1, f32[3072,1536]{1,0:T(8,128)} %trailing.1, f32[192,256]{1,0:T(8,128)} %first.1, f32[192,256]{1,0:T(8,128)} %second.1, f32[256,256]{1,0:T(8,128)} %link_in.1, ...), custom_call_target="tpu_custom_call" | custom-call | tf_op jit(solution)/shard_map/selected_inversion/pallas_call | solution.py:555
  89.1 2.1 %write_out.1 = (f32[192,256]{1,0:T(8,128)}, f32[256,256]{1,0:T(8,128)}, f32[192,256]{1,0:T(8,128)}, f32[256,256]{1,0:T(8,128)}, f32[256,256]{1,0:T(8,128)}) custom-call(f32[192,256]{1,0:T(8,128)} %get-tuple-element.10.refs_0_, f32[256,256]{1,0:T(8,128)} %get-tuple-element.11.refs_1_, f32[192,256]{1,0:T(8,128)} %get-tuple-element.12.refs_2_, ...), custom_call_target="tpu_custom_call" | custom-call | tf_op jit(solution)/shard_map/write_out/pallas_call | solution.py:597

commit v4 on v3

--- a/solution.py
+++ b/solution.py
@@ -40,6 +40,10 @@
     return jnp.dot(left, right, preferred_element_type=jnp.float32)
 
 
+def three(left, right):
+    return (dot(left[0], right[0]) + dot(left[1], right[0])) + dot(left[0], right[1])
+
+
 def exact(left, right, contract=(1, 0)):
     return lax.dot_general(
         left,
@@ -54,10 +58,10 @@
     struct, trailing, first, second, link_in, inv1_in, inv2_in,
     out1, diag1, out2, cross2, diag2,
     t_buf, raw, lead_h, lead_l, prod_a, prod_b, got_a, got_b, far_a, far_b,
-    lead, link, inv1, inv2, y_buf,
+    lead, near_lead, turned_h, turned_l, link, link_h, link_l, knil_h, knil_l, inv1, inv2, y_buf,
     sums, sum_p, sum_x, sum_q, total, tail, tail_p, tail_q, tail_x, last, tall, square,
     t_sem, in_sem, g1_send, g1_recv, g2_send, g2_recv, g3_send, g3_recv,
-    r_send, r_recv, f_send, f_recv, s_send, s_recv, e_send, e_recv, out_sem,
+    n_sem, r_send, r_recv, f_send, f_recv, s_send, s_recv, e_send, e_recv, out_sem,
 ):
     x, k, z, y = (lax.axis_index(name) for name in AXES)
     c = z * 4 + y
@@ -206,6 +210,25 @@
                 lead_h[p, rows] = high
                 lead_l[p, rows] = low
 
+    def share(slot):
+        far = slot % 3 + 1
+        where = at(dz=4 - far) if slot < 3 else at(dy=4 - far)
+        return remote(second, near_lead.at[slot], n_sem.at[0], n_sem.at[1], where)
+
+    def share_done():
+        remote(near_lead, near_lead, n_sem.at[0], n_sem.at[1], at(dk=1)).wait_recv()
+        for slot in range(6):
+            far = slot % 3 + 1
+            place = lax.rem(z + far, 4) * 4 + y if slot < 3 else z * 4 + lax.rem(y + far, 4)
+            for s in range(3):
+                part = pl.ds(64 * s, 64)
+                mask = struct[1, lax.div(((x * 2 + k) * 16 + place) * 3 + s, 2)].astype(jnp.float32)
+                near_lead[slot, part] = near_lead[slot, part] * mask
+        for slot in range(7):
+            turned_h[slot], turned_l[slot] = split(jnp.transpose(lead[1] if slot == 6 else near_lead[slot]))
+        link_h[...], link_l[...] = split(link[...])
+        knil_h[...], knil_l[...] = split(jnp.transpose(link[...]))
+
     def pick(h):
         return (prod_a, got_a, far_a) if h == 0 else (prod_b, got_b, far_b)
 
@@ -268,6 +291,12 @@
 
     def second_send(p, h, m):
         prod, _, got = pick(h)
+        if p == 0:
+            far = m + 1
+            return remote(
+                prod.at[p, PLACE[unit_of(h, 0, far)]], got.at[p, m], f_send.at[p, h], f_recv.at[p, h, m],
+                next_to(h, far, phase=2),
+            )
         far, way, lo, n = ((2, 1, 0, 96), (2, -1, 96, 96), (1, 1, 0, ROWS), (3, -1, 0, ROWS))[m]
         part = pl.ds(lo, n)
         return remote(
@@ -277,32 +306,56 @@
 
     def second_wait(p, h, m):
         _, _, got = pick(h)
-        ref = got.at[p, max(0, m - 1), pl.ds(96 if m == 1 else 0, 96 if m < 2 else ROWS)]
+        if p == 0:
+            ref = got.at[p, m]
+        else:
+            ref = got.at[p, max(0, m - 1), pl.ds(96 if m == 1 else 0, 96 if m < 2 else ROWS)]
         remote(ref, ref, f_send.at[p, h], f_recv.at[p, h, m], next_to(h, 1, phase=2)).wait_recv()
 
     def second_phase(p, far):
         for h in range(2):
-            prod, got, last_got = pick(h)
+            prod, got, _ = pick(h)
             u = PLACE[unit_of(h, 0, far)]
             hop_wait(p, h, 1, far)
             hop_wait(p, h, 2, far)
             prod[p, u] = prod[p, u] + (got[p, 1, far] + got[p, 2, far])
-            if far == 2:
+            if p == 0 and far:
+                second_send(p, h, far - 1).start()
+            if p == 1 and far == 2:
                 second_send(p, h, 0).start()
                 second_send(p, h, 1).start()
-            if far in (1, 3):
-                m = far // 2
-                second_wait(p, h, m)
-                part = pl.ds(96 * m, 96)
-                prod[p, u, part] = prod[p, u, part] + last_got[p, 0, part]
-                second_send(p, h, 2 + m).start()
-
-    def finish(p, h):
-        prod, _, got = pick(h)
-        second_wait(p, h, 2)
-        second_wait(p, h, 3)
-        value = prod[p, PLACE[(0, 0)]] + (got[p, 1] + got[p, 2])
-        y_buf[p, :, pl.ds(h * HALF, HALF)] = value
+
+    def gain(far):
+        for h in range(2):
+            prod, _, _ = pick(h)
+            slot = 6 if far == 0 else far - 1 + 3 * h
+            part = three((turned_h[slot], turned_l[slot]), split(prod[1, PLACE[unit_of(h, 0, far)]]))
+            cols = pl.ds(h * HALF, HALF)
+            tail[:, cols] = part if far == 2 else tail[:, cols] + part
+
+    def pass_on(far):
+        m = far // 2
+        for h in range(2):
+            prod, _, got = pick(h)
+            u = PLACE[unit_of(h, 0, far)]
+            second_wait(1, h, m)
+            part = pl.ds(96 * m, 96)
+            prod[1, u, part] = prod[1, u, part] + got[1, 0, part]
+            second_send(1, h, 2 + m).start()
+
+    def finish(p):
+        for h in range(2):
+            prod, _, got = pick(h)
+            value = prod[p, PLACE[(0, 0)]]
+            if p == 0:
+                for m in range(3):
+                    second_wait(p, h, m)
+                value = (value + got[p, 0]) + (got[p, 1] + got[p, 2])
+            else:
+                second_wait(p, h, 2)
+                second_wait(p, h, 3)
+                value = value + (got[p, 1] + got[p, 2])
+            y_buf[p, :, pl.ds(h * HALF, HALF)] = value
 
     def rows(ref, start, size):
         return ref.at[pl.ds(pl.multiple_of(start, 8), size)]
@@ -397,10 +450,6 @@
         half = rows(last, core * HALF, HALF)
         return late_sent(half, half, 4, at(dk=1))
 
-    def tail_half(core):
-        side = lead[1, :, pl.ds(pl.multiple_of(core * HALF, HALF), HALF)]
-        rows(tail, core * HALF, HALF)[...] = exact(side, y_buf[1], (0, 0))
-
     def late(step):
         if step == 0:
             late_swap(1 - k).start()
@@ -436,69 +485,72 @@
         return pltpu.make_async_copy(src, dst, out_sem.at[i])
 
     gather_1(0)
+    gather_0(1)
+    for slot in (0, 3, 2, 5):
+        share(slot).start()
     gather_2(0)
-    gather_0(1)
+    for slot in (1, 4):
+        share(slot).start()
     gather_3(0)
     gather_4(0)
     gather_5(0)
+    gather_1(1)
     compute(0, 0, 4)
-    gather_1(1)
     compute(0, 4, 7)
+    gather_2(1)
     compute(0, 7, 12)
     joined(0, 2)
-    gather_2(1)
-    compute(0, 12, 16)
+    gather_3(1)
+    compute(0, 12, 14)
+    gather_4(1)
+    compute(0, 14, 16)
     joined(0, 3)
     joined(0, 1)
     joined(0, 0)
-    gather_3(1)
-    gather_4(1)
     gather_5(1)
     compute(1, 0, 4)
     second_phase(0, 2)
     compute(1, 4, 7)
+    second_phase(0, 3)
+    second_phase(0, 1)
     compute(1, 7, 12)
     joined(1, 2)
+    second_phase(0, 0)
     compute(1, 12, 16)
     joined(1, 3)
-    second_phase(0, 3)
-    second_phase(0, 1)
-    second_phase(0, 0)
     joined(1, 1)
     joined(1, 0)
-    second_phase(1, 2)
-    finish(0, 0)
-    finish(0, 1)
+    finish(0)
     for p in range(2):
         sums[pl.ds(p * W, W)] = exact(lead[p], y_buf[0], (0, 0))
     early(0)
+    share_done()
+    early(1)
+    second_phase(1, 2)
+    gain(2)
+    second_phase(1, 3)
+    gain(3)
+    second_phase(1, 1)
+    gain(1)
+    second_phase(1, 0)
+    gain(0)
+    late(0)
     tall[0] = -y_buf[0]
     out_copy(0).start()
-    early(1)
-    second_phase(1, 3)
-    second_phase(1, 1)
+    early(2)
+    late(1)
+    pass_on(3)
+    pass_on(1)
     tall[1] = exact(y_buf[0], link[...])
-    second_phase(1, 0)
-    early(2)
-    finish(1, 0)
-    finish(1, 1)
-    tail_half(1 - k)
-    late(0)
-    tail_half(k)
+    early(3)
+    late(2)
+    finish(1)
     tall[1] = tall[1] - y_buf[1]
     out_copy(2).start()
-    late(1)
-    early(3)
-    late(2)
+    late(3)
     early(4)
-    late(3)
     early(5)
-    early(6)
-    square[0] = inv1[...] + total[pl.ds(0, W)]
-    out_copy(1).start()
-    square[1] = jnp.transpose(total[pl.ds(W, W)]) - exact(square[0], link[...])
-    out_copy(3).start()
-    square[2] = (inv2[...] - exact(link[...], square[1], (0, 0))) - exact(total[pl.ds(W, W)], link[...])
+    late(4)
     for p in range(2):
 
         @pl.when(at_home)
@@ -517,19 +569,30 @@
             _, got, final = pick(h)
             remote(got.at[p], got.at[p], r_send.at[p, h], r_recv.at[p, h, 0, 0], at(dk=1)).wait_send()
             remote(final.at[p], final.at[p], f_send.at[p, h], f_recv.at[p, h, 0], at(dk=1)).wait_send()
-    for ref, i in ((sum_p, 0), (sum_x, 1), (sum_q, 2), (sum_q, 3), (sum_x, 4), (sum_p, 5)):
+    for ref, i in ((sum_p, 0), (sum_x, 1), (sum_q, 2), (sum_q, 3), (sum_x, 4)):
         sent(ref, ref, i, at(dk=1)).wait_send()
     for ref, i in ((tail_p, 0), (tail_q, 1), (tail_x.at[pl.ds(0, 3)], 2)):
         late_sent(ref, ref, i, at(dk=1)).wait_send()
-    for i in range(4):
+    late_sent(tail_q, tail_q, 3, at(dk=1)).wait_send()
+    remote(near_lead, near_lead, n_sem.at[0], n_sem.at[1], at(dk=1)).wait_send()
+    for i in (0, 2):
         out_copy(i).wait()
-    late(4)
+    early(6)
+    square[0] = inv1[...] + total[pl.ds(0, W)]
+    out_copy(1).start()
+    link_parts, cross_sum = (link_h[...], link_l[...]), total[pl.ds(W, W)]
+    square[1] = jnp.transpose(cross_sum) - three(split(square[0]), link_parts)
+    out_copy(3).start()
+    square[2] = (inv2[...] - three((knil_h[...], knil_l[...]), split(square[1]))) - three(
+        split(cross_sum), link_parts
+    )
     late(5)
     square[2] = square[2] + last[...]
     out_copy(4).start()
-    late_sent(tail_q, tail_q, 3, at(dk=1)).wait_send()
     late_back(k).wait_send()
-    out_copy(4).wait()
+    sent(sum_p, sum_p, 5, at(dk=1)).wait_send()
+    for i in (1, 3, 4):
+        out_copy(i).wait()
 
 
 def write_out(*refs):
@@ -569,7 +632,14 @@
             pltpu.VMEM((2, 3, *block), f32),
             pltpu.VMEM((2, 3, *block), f32),
             pltpu.VMEM((2, ROWS, W), f32),
+            pltpu.VMEM((6, ROWS, W), f32),
+            pltpu.VMEM((7, W, ROWS), bf16),
+            pltpu.VMEM((7, W, ROWS), bf16),
             pltpu.VMEM((W, W), f32),
+            pltpu.VMEM((W, W), bf16),
+            pltpu.VMEM((W, W), bf16),
+            pltpu.VMEM((W, W), bf16),
+            pltpu.VMEM((W, W), bf16),
             pltpu.VMEM((W, W), f32),
             pltpu.VMEM((W, W), f32),
             pltpu.VMEM((2, ROWS, W), f32),
@@ -586,7 +656,7 @@
             pltpu.VMEM((2, ROWS, W), f32),
             pltpu.VMEM((3, W, W), f32),
             dma((16,)), dma((5,)), dma((2,)), dma((2, 4)), dma((2,)), dma((2, 2, 6)), dma((2,)), dma((2,)),
-            dma((2, 2)), dma((2, 2, 3, 4)), dma((2, 2)), dma((2, 2, 4)), dma((6,)), dma((6,)), dma((5,)), dma((5,)),
+            dma((2,)), dma((2, 2)), dma((2, 2, 3, 4)), dma((2, 2)), dma((2, 2, 4)), dma((6,)), dma((6,)), dma((5,)), dma((5,)),
             dma((5,)),
         ],
         compiler_params=pltpu.CompilerParams(

time: 91.5 us -> 88.4 us (0.966)
  Pallas kernels: 90.6 us -> 87.6 us
    pallas_call x1, Pallas kernels: 88.5 us -> 85.5 us  [on_device(): pl.pallas_call(kernel, out_shape=(tall, square, tall, square, square), in...]
where the time goes in v4:
time: 88.4 us; the launch traced here: 88.2 us
  Pallas kernels  87.6 us (99%)
    pallas_call x1, Pallas kernels, on_device(): pl.pallas_call(kernel, out_shape=(tall, square, tall, square, square), in...  85.5 us
    pallas_call x1, Pallas kernels, on_device(): pl.pallas_call(write_out, out_shape=(tall, square, tall, square, square),...  2.1 us

profile of v4, /device:TPU:1, one launch (start us, length us, event | category | flops | bytes accessed | tf_op | source)
XLA Modules:
  0.0 88.2 jit_solution(5930024986185428267)
XLA Ops:
  0.6 85.5 %selected_inversion.1 = (f32[192,256]{1,0:T(8,128)}, f32[256,256]{1,0:T(8,128)}, f32[192,256]{1,0:T(8,128)}, f32[256,256]{1,0:T(8,128)}, f32[256,256]{1,0:T(8,128)}) custom-call(s32[2,192]{1,0:T(2,128)} %struct.1, f32[3072,1536]{1,0:T(8,128)} %trailing.1, f32[192,256]{1,0:T(8,128)} %first.1, f32[192,256]{1,0:T(8,128)} %second.1, f32[256,256]{1,0:T(8,128)} %link_in.1, ...), custom_call_target="tpu_custom_call" | custom-call | tf_op jit(solution)/shard_map/selected_inversion/pallas_call | solution.py:618
  86.1 2.1 %write_out.1 = (f32[192,256]{1,0:T(8,128)}, f32[256,256]{1,0:T(8,128)}, f32[192,256]{1,0:T(8,128)}, f32[256,256]{1,0:T(8,128)}, f32[256,256]{1,0:T(8,128)}) custom-call(f32[192,256]{1,0:T(8,128)} %get-tuple-element.10.refs_0_, f32[256,256]{1,0:T(8,128)} %get-tuple-element.11.refs_1_, f32[192,256]{1,0:T(8,128)} %get-tuple-element.12.refs_2_, ...), custom_call_target="tpu_custom_call" | custom-call | tf_op jit(solution)/shard_map/write_out/pallas_call | solution.py:667

commit v5 on v4

--- a/solution.py
+++ b/solution.py
@@ -156,15 +156,17 @@
 
     passed = ((0, 3), (1, 2))
 
+    def ring_sem(way, m):
+        return 3 if m > 3 else (passed[way].index(m) if m in passed[way] else 2)
+
     def ring(p, way, m):
         step = 1 if way == 0 else -1
         ref = piece(p, m, 0) if m < 4 else piece(p, passed[way][m - 4], -step)
-        return remote(ref, ref, g2_send.at[p], g2_recv.at[p, way, m], at(dx=step))
-
-    def ring_wait(p, way, m):
-        step = 1 if way == 0 else -1
-        ref = piece(p, m, -step) if m < 4 else piece(p, passed[way][m - 4], -2 * step)
-        remote(ref, ref, g2_send.at[p], g2_recv.at[p, way, m], at(dx=step)).wait_recv()
+        return remote(ref, ref, g2_send.at[p], g2_recv.at[p, way, ring_sem(way, m)], at(dx=step))
+
+    def ring_wait(p, way, i):
+        ref = raw.at[p, 0, pl.ds(0, 48 if i < 2 else 96)]
+        remote(ref, ref, g2_send.at[p], g2_recv.at[p, way, i], at(dk=1)).wait_recv()
 
     def across(p, m):
         q = lax.rem(x + (0, -1, 1, 2)[m] + 4, 4)
@@ -182,19 +184,17 @@
     def gather_2(p):
         for m in range(2):
             for way in range(2):
-                ring_wait(p, way, passed[way][m])
+                ring_wait(p, way, m)
                 ring(p, way, 4 + m).start()
 
     def gather_3(p):
         for way in range(2):
-            for d in passed[1 - way]:
-                ring_wait(p, way, d)
+            ring_wait(p, way, 2)
             across(p, 1 + way).start()
 
     def gather_4(p):
         for way in range(2):
-            for m in (4, 5):
-                ring_wait(p, way, m)
+            ring_wait(p, way, 3)
         across(p, 3).start()
 
     def gather_5(p):
@@ -224,8 +224,9 @@
                 part = pl.ds(64 * s, 64)
                 mask = struct[1, lax.div(((x * 2 + k) * 16 + place) * 3 + s, 2)].astype(jnp.float32)
                 near_lead[slot, part] = near_lead[slot, part] * mask
-        for slot in range(7):
-            turned_h[slot], turned_l[slot] = split(jnp.transpose(lead[1] if slot == 6 else near_lead[slot]))
+        for slot in range(8):
+            rows_in = near_lead[slot] if slot < 6 else lead[7 - slot]
+            turned_h[slot], turned_l[slot] = split(jnp.transpose(rows_in))
         link_h[...], link_l[...] = split(link[...])
         knil_h[...], knil_l[...] = split(jnp.transpose(link[...]))
 
@@ -246,14 +247,13 @@
         prod, got, _ = pick(h)
         slot = 0 if kind == "relay" else (1 if way == 1 else 2)
         return remote(
-            prod.at[p, PLACE[unit]], got.at[p, slot, far], r_send.at[p, h], r_recv.at[p, h, slot, far],
+            prod.at[p, PLACE[unit]], got.at[p, slot, far], r_send.at[p, h], r_recv.at[p, min(slot, 1), far],
             next_to(h, way),
         )
 
-    def hop_wait(p, h, slot, far):
-        _, got, _ = pick(h)
-        ref = got.at[p, slot, far]
-        remote(ref, ref, r_send.at[p, h], r_recv.at[p, h, slot, far], next_to(h, 1)).wait_recv()
+    def hop_wait(p, kind, far):
+        ref = got_a.at[p, 0] if kind else got_a.at[p, pl.ds(0, 2), far]
+        remote(ref, ref, r_send.at[p, 0], r_recv.at[p, kind, far], at(dk=1)).wait_recv()
 
     def unit_of(h, near, far):
         return (near, far) if h == 0 else (far, near)
@@ -282,10 +282,10 @@
                             hop(p, h, UNITS[v]).start()
 
     def joined(p, far):
+        hop_wait(p, 0, far)
         for h in range(2):
             prod, got, _ = pick(h)
             unit = unit_of(h, 1 if far % 2 == 0 else 3, far)
-            hop_wait(p, h, 0, far)
             prod[p, PLACE[unit]] = prod[p, PLACE[unit]] + got[p, 0, far]
             hop(p, h, unit).start()
 
@@ -294,30 +294,28 @@
         if p == 0:
             far = m + 1
             return remote(
-                prod.at[p, PLACE[unit_of(h, 0, far)]], got.at[p, m], f_send.at[p, h], f_recv.at[p, h, m],
+                prod.at[p, PLACE[unit_of(h, 0, far)]], got.at[p, m], f_send.at[p, h], f_recv.at[p, 0],
                 next_to(h, far, phase=2),
             )
         far, way, lo, n = ((2, 1, 0, 96), (2, -1, 96, 96), (1, 1, 0, ROWS), (3, -1, 0, ROWS))[m]
         part = pl.ds(lo, n)
         return remote(
             prod.at[p, PLACE[unit_of(h, 0, far)], part], got.at[p, max(0, m - 1), part], f_send.at[p, h],
-            f_recv.at[p, h, m], next_to(h, way, phase=2),
+            f_recv.at[p, min(m, 2)], next_to(h, way, phase=2),
         )
 
-    def second_wait(p, h, m):
-        _, _, got = pick(h)
-        if p == 0:
-            ref = got.at[p, m]
+    def second_wait(p, m):
+        if m < 2:
+            ref = far_a.at[p, 0]
         else:
-            ref = got.at[p, max(0, m - 1), pl.ds(96 if m == 1 else 0, 96 if m < 2 else ROWS)]
-        remote(ref, ref, f_send.at[p, h], f_recv.at[p, h, m], next_to(h, 1, phase=2)).wait_recv()
+            ref = got_a.at[p, pl.ds(0, 2), pl.ds(0, 3)] if p == 0 else got_a.at[p, 0]
+        remote(ref, ref, f_send.at[p, 0], f_recv.at[p, m if p else 0], at(dk=1)).wait_recv()
 
     def second_phase(p, far):
+        hop_wait(p, 1, far)
         for h in range(2):
             prod, got, _ = pick(h)
             u = PLACE[unit_of(h, 0, far)]
-            hop_wait(p, h, 1, far)
-            hop_wait(p, h, 2, far)
             prod[p, u] = prod[p, u] + (got[p, 1, far] + got[p, 2, far])
             if p == 0 and far:
                 second_send(p, h, far - 1).start()
@@ -335,25 +333,22 @@
 
     def pass_on(far):
         m = far // 2
+        second_wait(1, m)
         for h in range(2):
             prod, _, got = pick(h)
             u = PLACE[unit_of(h, 0, far)]
-            second_wait(1, h, m)
             part = pl.ds(96 * m, 96)
             prod[1, u, part] = prod[1, u, part] + got[1, 0, part]
             second_send(1, h, 2 + m).start()
 
     def finish(p):
+        second_wait(p, 2)
         for h in range(2):
             prod, _, got = pick(h)
             value = prod[p, PLACE[(0, 0)]]
             if p == 0:
-                for m in range(3):
-                    second_wait(p, h, m)
                 value = (value + got[p, 0]) + (got[p, 1] + got[p, 2])
             else:
-                second_wait(p, h, 2)
-                second_wait(p, h, 3)
                 value = value + (got[p, 1] + got[p, 2])
             y_buf[p, :, pl.ds(h * HALF, HALF)] = value
 
@@ -520,14 +515,15 @@
     joined(1, 3)
     joined(1, 1)
     joined(1, 0)
+    share_done()
     finish(0)
+    y_parts = split(y_buf[0])
     for p in range(2):
-        sums[pl.ds(p * W, W)] = exact(lead[p], y_buf[0], (0, 0))
+        sums[pl.ds(p * W, W)] = three((turned_h[7 - p], turned_l[7 - p]), y_parts)
     early(0)
-    share_done()
-    early(1)
     second_phase(1, 2)
     gain(2)
+    early(1)
     second_phase(1, 3)
     gain(3)
     second_phase(1, 1)
@@ -567,8 +563,8 @@
         remote(sixteen, sixteen, g3_send.at[p], g3_recv.at[p], at(dk=1)).wait_send()
         for h in range(2):
             _, got, final = pick(h)
-            remote(got.at[p], got.at[p], r_send.at[p, h], r_recv.at[p, h, 0, 0], at(dk=1)).wait_send()
-            remote(final.at[p], final.at[p], f_send.at[p, h], f_recv.at[p, h, 0], at(dk=1)).wait_send()
+            remote(got.at[p], got.at[p], r_send.at[p, h], r_recv.at[p, 0, 0], at(dk=1)).wait_send()
+            remote(final.at[p], final.at[p], f_send.at[p, h], f_recv.at[p, 0], at(dk=1)).wait_send()
     for ref, i in ((sum_p, 0), (sum_x, 1), (sum_q, 2), (sum_q, 3), (sum_x, 4)):
         sent(ref, ref, i, at(dk=1)).wait_send()
     for ref, i in ((tail_p, 0), (tail_q, 1), (tail_x.at[pl.ds(0, 3)], 2)):
@@ -633,8 +629,8 @@
             pltpu.VMEM((2, 3, *block), f32),
             pltpu.VMEM((2, ROWS, W), f32),
             pltpu.VMEM((6, ROWS, W), f32),
-            pltpu.VMEM((7, W, ROWS), bf16),
-            pltpu.VMEM((7, W, ROWS), bf16),
+            pltpu.VMEM((8, W, ROWS), bf16),
+            pltpu.VMEM((8, W, ROWS), bf16),
             pltpu.VMEM((W, W), f32),
             pltpu.VMEM((W, W), bf16),
             pltpu.VMEM((W, W), bf16),
@@ -655,8 +651,8 @@
             pltpu.VMEM((W, W), f32),
             pltpu.VMEM((2, ROWS, W), f32),
             pltpu.VMEM((3, W, W), f32),
-            dma((16,)), dma((5,)), dma((2,)), dma((2, 4)), dma((2,)), dma((2, 2, 6)), dma((2,)), dma((2,)),
-            dma((2,)), dma((2, 2)), dma((2, 2, 3, 4)), dma((2, 2)), dma((2, 2, 4)), dma((6,)), dma((6,)), dma((5,)), dma((5,)),
+            dma((16,)), dma((5,)), dma((2,)), dma((2, 4)), dma((2,)), dma((2, 2, 4)), dma((2,)), dma((2,)),
+            dma((2,)), dma((2, 2)), dma((2, 2, 4)), dma((2, 2)), dma((2, 3)), dma((6,)), dma((6,)), dma((5,)), dma((5,)),
             dma((5,)),
         ],
         compiler_params=pltpu.CompilerParams(

time: 88.4 us -> 87.9 us (level)
  no operation moved by 1% of the time
where the time goes in v5:
time: 87.9 us; the launch traced here: 87.7 us
  Pallas kernels  87 us (99%)
    pallas_call x1, Pallas kernels, on_device(): pl.pallas_call(kernel, out_shape=(tall, square, tall, square, square), in...  84.9 us
    pallas_call x1, Pallas kernels, on_device(): pl.pallas_call(write_out, out_shape=(tall, square, tall, square, square),...  2.1 us

profile of v5, /device:TPU:1, one launch (start us, length us, event | category | flops | bytes accessed | tf_op | source)
XLA Modules:
  0.0 87.7 jit_solution(12519187003419552189)
XLA Ops:
  0.6 84.9 %selected_inversion.1 = (f32[192,256]{1,0:T(8,128)}, f32[256,256]{1,0:T(8,128)}, f32[192,256]{1,0:T(8,128)}, f32[256,256]{1,0:T(8,128)}, f32[256,256]{1,0:T(8,128)}) custom-call(s32[2,192]{1,0:T(2,128)} %struct.1, f32[3072,1536]{1,0:T(8,128)} %trailing.1, f32[192,256]{1,0:T(8,128)} %first.1, f32[192,256]{1,0:T(8,128)} %second.1, f32[256,256]{1,0:T(8,128)} %link_in.1, ...), custom_call_target="tpu_custom_call" | custom-call | tf_op jit(solution)/shard_map/selected_inversion/pallas_call | solution.py:614
  85.6 2.1 %write_out.1 = (f32[192,256]{1,0:T(8,128)}, f32[256,256]{1,0:T(8,128)}, f32[192,256]{1,0:T(8,128)}, f32[256,256]{1,0:T(8,128)}, f32[256,256]{1,0:T(8,128)}) custom-call(f32[192,256]{1,0:T(8,128)} %get-tuple-element.10.refs_0_, f32[256,256]{1,0:T(8,128)} %get-tuple-element.11.refs_1_, f32[192,256]{1,0:T(8,128)} %get-tuple-element.12.refs_2_, ...), custom_call_target="tpu_custom_call" | custom-call | tf_op jit(solution)/shard_map/write_out/pallas_call | solution.py:663
